TPU v7x, 512 devices: a whole 4x8x8 slice. The times are simulated.
512 devices in a mesh: dp: 16 (over y, core), space: 32 (over z, x).
Axes of the slice: x: 4, y: 8, z: 8, core: 2. Of those that a mesh axis runs over, the one named last changes fastest.
Arguments:
- latent: bfloat16 [16, 256, 64, 320], P('dp', 'space'), may hold values from -6 to 6
- first_weight: bfloat16 [320, 3, 3, 320], replicated, may hold values from -0.109375 to 0.109375
- second_weight: bfloat16 [320, 3, 3, 320], replicated, may hold values from -0.109375 to 0.109375
- cotangent: bfloat16 [16, 256, 64, 320], P('dp', 'space'), may hold values from -6 to 6
Outputs:
- output_map: bfloat16 [16, 256, 64, 320], P('dp', 'space')
- latent_grad: bfloat16 [16, 256, 64, 320], P('dp', 'space')
- first_grad: float32 [921600], P(('dp', 'space'))
- second_grad: float32 [921600], P(('dp', 'space'))
All inputs are finite; a program needn't handle non-finite values.
Results may differ from a plain program's by a relative error of at most 0.017.
Values may be sent and summed in bfloat16 or wider, within the bound.
A program may use at most 128 MiB of HBM per device.

v0:
```python
import jax
import jax.numpy as jnp
from jax import lax
from jax.sharding import PartitionSpec as P


def extended(cells, sides, width):
    for axis, dim in sides:
        count = lax.axis_size(axis)
        ends = count - 1
        head = lax.slice_in_dim(cells, 0, width, axis=dim)
        tail = lax.slice_in_dim(cells, cells.shape[dim] - width, cells.shape[dim], axis=dim)
        cells = jnp.concatenate(
            [
                lax.ppermute(tail, axis, [(i, (i + 1) % count) for i in range(ends)]),
                cells,
                lax.ppermute(head, axis, [((i + 1) % count, i) for i in range(ends)]),
            ],
            axis=dim,
        )
    return cells


def silu_value(value):
    return value * jax.nn.sigmoid(value)


def silu_slope(value):
    sig = jax.nn.sigmoid(value)
    return sig * (1.0 + value * (1.0 - sig))


def pad_cols(field):
    return jnp.pad(field, ((0, 0), (1, 1), (0, 0)))


def conv_sum(padded, weight, row_count, col_count, flip, weight_dim):
    total = None
    for i in range(3):
        for j in range(3):
            start_row = 2 - i if flip else i
            start_col = 2 - j if flip else j
            piece = padded[start_row : start_row + row_count, start_col : start_col + col_count]
            piece = piece.reshape(row_count * col_count, padded.shape[2])
            term = lax.dot_general(
                piece,
                weight[:, i, j, :],
                (((1,), (weight_dim,)), ((), ())),
                preferred_element_type=jnp.float32,
            )
            total = term if total is None else total + term
    return total


def weight_terms(padded, other, row_count, col_count, first):
    pieces = []
    for i in range(3):
        for j in range(3):
            piece = padded[i : i + row_count, j : j + col_count].reshape(
                row_count * col_count, padded.shape[2]
            )
            if first:
                term = lax.dot_general(
                    piece, other, (((0,), (0,)), ((), ())), preferred_element_type=jnp.float32
                )
            else:
                term = lax.dot_general(
                    other, piece, (((0,), (0,)), ((), ())), preferred_element_type=jnp.float32
                )
            pieces.append(term)
    return jnp.concatenate(pieces, axis=1).reshape(-1)


def local(latent, first_weight, second_weight, cotangent):
    sample = latent[0]
    row_count, col_count, chans = sample.shape
    mids = first_weight.shape[3]
    active = silu_value(sample.astype(jnp.float32)).astype(jnp.bfloat16)
    active_pad = pad_cols(extended(active, (("space", 0),), 1))
    hidden = conv_sum(active_pad, first_weight, row_count, col_count, False, 0).astype(jnp.bfloat16)
    hidden_act = (
        silu_value(hidden.astype(jnp.float32))
        .astype(jnp.bfloat16)
        .reshape(row_count, col_count, mids)
    )
    hidden_pad = pad_cols(extended(hidden_act, (("space", 0),), 1))
    output_map = conv_sum(hidden_pad, second_weight, row_count, col_count, False, 1).astype(
        jnp.bfloat16
    )
    grad_out = cotangent[0]
    grad_flat = grad_out.reshape(row_count * col_count, chans)
    second_term = weight_terms(hidden_pad, grad_flat, row_count, col_count, False)
    grad_pad = pad_cols(extended(grad_out, (("space", 0),), 1))
    hidden_back = conv_sum(grad_pad, second_weight, row_count, col_count, True, 0)
    hidden_grad = (hidden_back * silu_slope(hidden.astype(jnp.float32))).astype(jnp.bfloat16)
    first_term = weight_terms(active_pad, hidden_grad, row_count, col_count, True)
    back_pad = pad_cols(
        extended(hidden_grad.reshape(row_count, col_count, mids), (("space", 0),), 1)
    )
    active_back = conv_sum(back_pad, first_weight, row_count, col_count, True, 1)
    latent_grad = (
        active_back * silu_slope(sample.reshape(row_count * col_count, chans).astype(jnp.float32))
    ).astype(jnp.bfloat16)
    data_count = lax.axis_size("dp")
    space_count = lax.axis_size("space")
    share = first_term.shape[0] // (data_count * space_count)
    first_grid = first_term.reshape(data_count, space_count, share)
    second_grid = second_term.reshape(data_count, space_count, share)
    recv_first, recv_second = (
        lax.all_to_all(
            first_grid.astype(jnp.bfloat16), "space", split_axis=1, concat_axis=1, tiled=True
        ).astype(first_grid.dtype),
        lax.all_to_all(
            second_grid.astype(jnp.bfloat16), "space", split_axis=1, concat_axis=1, tiled=True
        ).astype(second_grid.dtype),
    )
    summed_first = jnp.sum(recv_first, axis=1)
    summed_second = jnp.sum(recv_second, axis=1)
    last_first, last_second = (
        lax.all_to_all(
            summed_first.astype(jnp.bfloat16), "dp", split_axis=0, concat_axis=0, tiled=True
        ).astype(summed_first.dtype),
        lax.all_to_all(
            summed_second.astype(jnp.bfloat16), "dp", split_axis=0, concat_axis=0, tiled=True
        ).astype(summed_second.dtype),
    )
    first_grad = jnp.sum(last_first, axis=0)
    second_grad = jnp.sum(last_second, axis=0)
    return (
        output_map.reshape(1, row_count, col_count, chans),
        latent_grad.reshape(1, row_count, col_count, chans),
        first_grad,
        second_grad,
    )


def solution(mesh):
    placed = (P("dp", "space", None, None), P(), P(), P("dp", "space", None, None))
    return jax.shard_map(
        local,
        mesh=mesh,
        in_specs=placed,
        out_specs=(
            P("dp", "space", None, None),
            P("dp", "space", None, None),
            P(("dp", "space")),
            P(("dp", "space")),
        ),
        check_vma=False,
    )
```

profile of v0, /device:TPU:1, one launch (start us, length us, event | category | flops | bytes accessed | tf_op | source)
XLA Modules:
  0.0 222.1 jit_solution(11894396203343919044)
XLA Ops:
  1.6 3.9 %collective-permute-start.4 = (bf16[1,64,320]{2,1,0:T(8,128)(2,1)S(1)}, bf16[1,64,320]{2,1,0:T(8,128)(2,1)S(1)}, u32[]{:S(2)}, u32[]{:S(2)}) collective-permute-start(bf16[1,64,320]{2,1,0:T(8,128)(2,1)S(1)} %get-tuple-element.36), channel_id=1, source_target_pairs={{0,1},{1,2},{2,3},{3,4},{4,5},{5,6},{6,7},{7,8},{8,9},{9,10},{10,1... | collective-permute-start | bytes 122888 | tf_op jit(solution)/shard_map/ppermute | solution.py:15
  5.5 1.3 collective-permute-start.5
  6.8 1.2 fusion.26
  8.7 4.0 %collective-permute-start = (bf16[1,64,320]{2,1,0:T(8,128)(2,1)}, bf16[1,64,320]{2,1,0:T(8,128)(2,1)S(1)}, u32[]{:S(2)}, u32[]{:S(2)}) collective-permute-start(bf16[1,64,320]{2,1,0:T(8,128)(2,1)} %get-tuple-element.42), channel_id=1, source_target_pairs={{0,1},{1,2},{2,3},{3,4},{4,5},{5,6},{6,7},{7,8},{8,9},{9,10},{10,1... | collective-permute-start | bytes 122888 | tf_op jit(solution)/shard_map/ppermute | solution.py:15
  12.7 1.3 collective-permute-start.1
  14.0 1.2 multiply_convert_fusion
  15.2 1.1 copy.62
  17.5 1.2 copy-done.1
  20.1 1.2 copy-done.2
  28.0 1.1 convolution_convert_fusion.10
  29.1 1.1 convolution_convert_fusion.11
  30.2 1.1 convolution_convert_fusion.12
  31.3 1.1 convolution_convert_fusion.14
  32.4 1.1 convolution_convert_fusion.15
  33.5 1.1 convolution_convert_fusion.16
  34.6 1.1 convolution_convert_fusion.17
  35.7 1.1 convolution_convert_fusion.9
  40.6 4.6 %collective-permute-start.6 = (bf16[1,64,320]{1,2,0:T(8,128)(2,1)}, bf16[1,64,320]{1,2,0:T(8,128)(2,1)}, u32[]{:S(2)}, u32[]{:S(2)}) collective-permute-start(bf16[1,64,320]{1,2,0:T(8,128)(2,1)} %get-tuple-element.44), channel_id=1, source_target_pairs={{0,1},{1,2},{2,3},{3,4},{4,5},{5,6},{6,7},{7,8},{8,9},{9,10},{10,1... | collective-permute-start | bytes 122888 | tf_op jit(solution)/shard_map/ppermute | solution.py:15
  45.2 1.3 collective-permute-start.7
  46.5 4.6 %collective-permute-start.2 = (bf16[1,64,320]{1,2,0:T(8,128)(2,1)}, bf16[1,64,320]{1,2,0:T(8,128)(2,1)}, u32[]{:S(2)}, u32[]{:S(2)}) collective-permute-start(bf16[1,64,320]{1,2,0:T(8,128)(2,1)} %get-tuple-element.46), channel_id=1, source_target_pairs={{0,1},{1,2},{2,3},{3,4},{4,5},{5,6},{6,7},{7,8},{8,9},{9,10},{10,1... | collective-permute-start | bytes 122888 | tf_op jit(solution)/shard_map/ppermute | solution.py:15
  51.1 1.5 collective-permute-start.3
  52.6 2.1 convolution_convert_fusion.13
  54.7 4.1 %concatenate.56 = bf16[320,2880]{1,0:T(8,128)(2,1)} concatenate(bf16[320,320]{1,0:T(8,128)(2,1)} %convolution_convert_fusion.17, bf16[320,320]{1,0:T(8,128)(2,1)} %convolution_convert_fusion.16, bf16[320,320]{1,0:T(8,128)(2,1)} %convolution_convert_fusion.15, bf16[320,320]{1,0:T(8,128)(2,1)} %convolution_convert_fusion.14, bf16[320,320]{1,0:T(8,128)(2,1)} %convolution_convert_fusion.13, ...), dimensions={1} | concatenate | bytes 3686400 | tf_op jit(solution)/shard_map/concatenate | solution.py:71
  58.8 5.5 %convert_element_type.86 = bf16[16,32,1800]{2,1,0:T(8,128)(2,1)} reshape(bf16[320,2880]{1,0:T(8,128)(2,1)} %concatenate.56) | data formatting | bytes 3686400 | tf_op jit(solution)/shard_map/convert_element_type | solution.py:111
  64.3 3.4 %copy.66 = bf16[16,32,1800]{2,0,1:T(8,128)(2,1)} copy(bf16[16,32,1800]{2,1,0:T(8,128)(2,1)} %convert_element_type.86) | data formatting | bytes 3686400 | tf_op jit(solution)/shard_map/convert_element_type | solution.py:111
  67.7 23.4 %all-to-all-start = ((bf16[16,32,1800]{2,0,1:T(8,128)(2,1)}), bf16[16,32,1800]{2,0,1:T(8,128)(2,1)}, u32[]{:S(2)}, u32[]{:S(2)}) async-start(bf16[16,32,1800]{2,0,1:T(8,128)(2,1)} %copy.66), calls=%async_computation | async-start | bytes 3932160 | tf_op jit(solution)/shard_map/all_to_all | solution.py:110
  91.1 1.0 copy.52
  92.1 1.6 copy.53
  93.7 1.2 select_maximum_fusion.4
  94.9 1.3 pad_maximum_fusion.4
  96.1 1.1 fusion.14
  97.2 1.1 fusion.20
  98.7 1.4 fusion.19
  100.1 1.1 fusion.21
  101.2 1.1 fusion.18
  102.3 1.1 fusion.16
  103.4 1.1 fusion.15
  104.5 1.1 fusion.13
  105.6 4.0 %concatenate.57 = bf16[320,2880]{1,0:T(8,128)(2,1)} concatenate(bf16[320,320]{1,0:T(8,128)(2,1)} %fusion.13, bf16[320,320]{1,0:T(8,128)(2,1)} %fusion.14, bf16[320,320]{1,0:T(8,128)(2,1)} %fusion.15, bf16[320,320]{1,0:T(8,128)(2,1)} %fusion.16, bf16[320,320]{1,0:T(8,128)(2,1)S(1)} %fusion.17, bf16[320,320]{1,0:T(8,128)(2,1)} %fusion.18, bf16[320,320]{1,0:T(8,128)(2,1)} %fusion.19, ...), dimensions={1} | concatenate | bytes 3686400 | tf_op jit(solution)/shard_map/concatenate | solution.py:71
  109.6 5.5 %convert_element_type.88 = bf16[16,32,1800]{2,1,0:T(8,128)(2,1)} reshape(bf16[320,2880]{1,0:T(8,128)(2,1)} %concatenate.57) | data formatting | bytes 3686400 | tf_op jit(solution)/shard_map/convert_element_type | solution.py:114
  115.2 3.4 %copy.68 = bf16[16,32,1800]{2,0,1:T(8,128)(2,1)} copy(bf16[16,32,1800]{2,1,0:T(8,128)(2,1)} %convert_element_type.88) | data formatting | bytes 3686400 | tf_op jit(solution)/shard_map/convert_element_type | solution.py:114
  118.6 1.0 copy.58
  119.6 1.0 copy.59
  120.6 1.2 select_maximum_fusion
  121.8 2.1 pad_maximum_fusion
  124.0 2.2 fusion.53
  126.2 2.2 %fusion.41 = f32[512,320]{0,1:T(8,128)} fusion(bf16[512,320]{1,0:T(8,128)(2,1)} %bitcast.271, bf16[320,3,3,320]{3,0,2,1:T(8,128)(2,1)S(1)} %copy-done.1), kind=kOutput, calls=%fused_computation.108 | convolution fusion | flops 104857600 | bytes 1228800 | tf_op jit(solution)/shard_map/dot_general | solution.py:45
  128.4 1.2 fusion.38
  129.6 1.3 fusion.115
  130.9 2.2 fusion.60
  133.6 9.0 %all-to-all-start.2 = ((bf16[16,32,1800]{2,0,1:T(8,128)(2,1)}), bf16[16,32,1800]{2,0,1:T(8,128)(2,1)}, u32[]{:S(2)}, u32[]{:S(2)}) async-start(bf16[16,32,1800]{2,0,1:T(8,128)(2,1)} %copy.68), calls=%async_computation.2 | async-start | bytes 3932160 | tf_op jit(solution)/shard_map/all_to_all | solution.py:113
  142.6 1.5 fusion.63
  144.1 1.3 fusion.74
  147.6 1.2 convolution_add_fusion.15
  151.6 1.2 fusion.12
  152.8 1.9 reduce_sum.42
  156.6 28.3 %all-to-all-done.2 = bf16[16,32,1800]{2,0,1:T(8,128)(2,1)} async-done(((bf16[16,32,1800]{2,0,1:T(8,128)(2,1)}), bf16[16,32,1800]{2,0,1:T(8,128)(2,1)}, u32[]{:S(2)}, u32[]{:S(2)}) %all-to-all-start.2) | async-done | bytes 1843232 | tf_op jit(solution)/shard_map/all_to_all | solution.py:113
  185.0 13.1 %all-to-all-start.1 = ((bf16[16,2,900]{2,1,0:T(2,128)(2,1)}), bf16[16,2,900]{2,1,0:T(2,128)(2,1)S(1)}, u32[]{:S(2)}, u32[]{:S(2)}) async-start(bf16[16,2,900]{2,1,0:T(2,128)(2,1)} %reshape.202), calls=%async_computation.1 | async-start | bytes 131072 | tf_op jit(solution)/shard_map/all_to_all | solution.py:120
  198.1 1.1 fusion.10
  199.2 1.9 copy.64
  201.1 1.9 copy.56
  203.0 1.8 reduce_sum.44
  206.2 7.2 %all-to-all-start.3 = ((bf16[16,2,900]{2,1,0:T(2,128)(2,1)}), bf16[16,2,900]{2,1,0:T(2,128)(2,1)S(1)}, u32[]{:S(2)}, u32[]{:S(2)}) async-start(bf16[16,2,900]{2,1,0:T(2,128)(2,1)} %reshape.204), calls=%async_computation.3 | async-start | bytes 131072 | tf_op jit(solution)/shard_map/all_to_all | solution.py:123
  214.3 7.0 %all-to-all-done.3 = bf16[16,2,900]{2,1,0:T(2,128)(2,1)S(1)} async-done(((bf16[16,2,900]{2,1,0:T(2,128)(2,1)}), bf16[16,2,900]{2,1,0:T(2,128)(2,1)S(1)}, u32[]{:S(2)}, u32[]{:S(2)}) %all-to-all-start.3) | async-done | bytes 57632 | tf_op jit(solution)/shard_map/all_to_all | solution.py:123
  (122 shorter events, 25.2 us)
Async XLA Ops:
  0.6 16.3 %copy-start = (bf16[1,8,64,320]{3,2,1,0:T(8,128)(2,1)S(1)}, bf16[1,8,64,320]{3,2,1,0:T(8,128)(2,1)}, u32[]{:S(2)}) copy-start(bf16[1,8,64,320]{3,2,1,0:T(8,128)(2,1)} %param.7) | copy-start | bytes 983044
  0.6 14.6 %copy-start.4 = (bf16[1,8,64,320]{3,2,1,0:T(8,128)(2,1)S(1)}, bf16[1,8,64,320]{3,2,1,0:T(8,128)(2,1)}, u32[]{:S(2)}) copy-start(bf16[1,8,64,320]{3,2,1,0:T(8,128)(2,1)} %param.4) | copy-start | bytes 983044
  1.6 14.7 %collective-permute-start.4 = (bf16[1,64,320]{2,1,0:T(8,128)(2,1)S(1)}, bf16[1,64,320]{2,1,0:T(8,128)(2,1)S(1)}, u32[]{:S(2)}, u32[]{:S(2)}) collective-permute-start(bf16[1,64,320]{2,1,0:T(8,128)(2,1)S(1)} %get-tuple-element.36), channel_id=1, source_target_pairs={{0,1},{1,2},{2,3},{3,4},{4,5},{5,6},{6,7},{7,8},{8,9},{9,10},{10,1... | collective-permute-start | bytes 122888 | tf_op jit(solution)/shard_map/ppermute | solution.py:15
  5.5 10.8 %collective-permute-start.5 = (bf16[1,64,320]{2,1,0:T(8,128)(2,1)S(1)}, bf16[1,64,320]{2,1,0:T(8,128)(2,1)S(1)}, u32[]{:S(2)}, u32[]{:S(2)}) collective-permute-start(bf16[1,64,320]{2,1,0:T(8,128)(2,1)S(1)} %get-tuple-element.37), channel_id=1, source_target_pairs={{1,0},{2,1},{3,2},{4,3},{5,4},{6,5},{7,6},{8,7},{9,8},{10,9},{11,1... | collective-permute-start | bytes 122888 | tf_op jit(solution)/shard_map/ppermute | solution.py:17
  8.7 10.8 %collective-permute-start = (bf16[1,64,320]{2,1,0:T(8,128)(2,1)}, bf16[1,64,320]{2,1,0:T(8,128)(2,1)S(1)}, u32[]{:S(2)}, u32[]{:S(2)}) collective-permute-start(bf16[1,64,320]{2,1,0:T(8,128)(2,1)} %get-tuple-element.42), channel_id=1, source_target_pairs={{0,1},{1,2},{2,3},{3,4},{4,5},{5,6},{6,7},{7,8},{8,9},{9,10},{10,1... | collective-permute-start | bytes 122888 | tf_op jit(solution)/shard_map/ppermute | solution.py:15
  12.7 6.8 %collective-permute-start.1 = (bf16[1,64,320]{2,1,0:T(8,128)(2,1)}, bf16[1,64,320]{2,1,0:T(8,128)(2,1)S(1)}, u32[]{:S(2)}, u32[]{:S(2)}) collective-permute-start(bf16[1,64,320]{2,1,0:T(8,128)(2,1)} %get-tuple-element.43), channel_id=1, source_target_pairs={{1,0},{2,1},{3,2},{4,3},{5,4},{6,5},{7,6},{8,7},{9,8},{10,9},{11,1... | collective-permute-start | bytes 122888 | tf_op jit(solution)/shard_map/ppermute | solution.py:17
  16.3 0.6 copy-start.30
  17.1 1.6 copy-start.1
  19.7 1.6 copy-start.2
  20.1 2.0 copy-start.31
  40.6 78.1 %collective-permute-start.6 = (bf16[1,64,320]{1,2,0:T(8,128)(2,1)}, bf16[1,64,320]{1,2,0:T(8,128)(2,1)}, u32[]{:S(2)}, u32[]{:S(2)}) collective-permute-start(bf16[1,64,320]{1,2,0:T(8,128)(2,1)} %get-tuple-element.44), channel_id=1, source_target_pairs={{0,1},{1,2},{2,3},{3,4},{4,5},{5,6},{6,7},{7,8},{8,9},{9,10},{10,1... | collective-permute-start | bytes 122888 | tf_op jit(solution)/shard_map/ppermute | solution.py:15
  45.2 74.4 %collective-permute-start.7 = (bf16[1,64,320]{1,2,0:T(8,128)(2,1)}, bf16[1,64,320]{1,2,0:T(8,128)(2,1)}, u32[]{:S(2)}, u32[]{:S(2)}) collective-permute-start(bf16[1,64,320]{1,2,0:T(8,128)(2,1)} %get-tuple-element.45), channel_id=1, source_target_pairs={{1,0},{2,1},{3,2},{4,3},{5,4},{6,5},{7,6},{8,7},{9,8},{10,9},{11,1... | collective-permute-start | bytes 122888 | tf_op jit(solution)/shard_map/ppermute | solution.py:17
  46.5 44.6 %collective-permute-start.2 = (bf16[1,64,320]{1,2,0:T(8,128)(2,1)}, bf16[1,64,320]{1,2,0:T(8,128)(2,1)}, u32[]{:S(2)}, u32[]{:S(2)}) collective-permute-start(bf16[1,64,320]{1,2,0:T(8,128)(2,1)} %get-tuple-element.46), channel_id=1, source_target_pairs={{0,1},{1,2},{2,3},{3,4},{4,5},{5,6},{6,7},{7,8},{8,9},{9,10},{10,1... | collective-permute-start | bytes 122888 | tf_op jit(solution)/shard_map/ppermute | solution.py:15
  51.1 40.9 %collective-permute-start.3 = (bf16[1,64,320]{1,2,0:T(8,128)(2,1)}, bf16[1,64,320]{1,2,0:T(8,128)(2,1)}, u32[]{:S(2)}, u32[]{:S(2)}) collective-permute-start(bf16[1,64,320]{1,2,0:T(8,128)(2,1)} %get-tuple-element.47), channel_id=1, source_target_pairs={{1,0},{2,1},{3,2},{4,3},{5,4},{6,5},{7,6},{8,7},{9,8},{10,9},{11,1... | collective-permute-start | bytes 122888 | tf_op jit(solution)/shard_map/ppermute | solution.py:17
  67.7 65.9 %all-to-all-start = ((bf16[16,32,1800]{2,0,1:T(8,128)(2,1)}), bf16[16,32,1800]{2,0,1:T(8,128)(2,1)}, u32[]{:S(2)}, u32[]{:S(2)}) async-start(bf16[16,32,1800]{2,0,1:T(8,128)(2,1)} %copy.66), calls=%async_computation | async-start | bytes 3932160 | tf_op jit(solution)/shard_map/all_to_all | solution.py:110
  96.1 1.1 copy-start.15
  96.1 1.1 copy-start.17
  98.7 5.8 %copy-start.5 = (bf16[8,64,320]{2,1,0:T(8,128)(2,1)}, bf16[8,64,320]{2,1,0:T(8,128)(2,1)S(1)}, u32[]{:S(2)}) copy-start(bf16[8,64,320]{2,1,0:T(8,128)(2,1)S(1)} %get-tuple-element.20) | copy-start | bytes 983044
  98.7 5.8 %copy-start.7 = (bf16[8,64,320]{2,1,0:T(8,128)(2,1)}, bf16[8,64,320]{2,1,0:T(8,128)(2,1)S(1)}, u32[]{:S(2)}) copy-start(bf16[8,64,320]{2,1,0:T(8,128)(2,1)S(1)} %get-tuple-element.21) | copy-start | bytes 983044
  98.7 5.8 %copy-start.9 = (bf16[8,64,320]{2,1,0:T(8,128)(2,1)}, bf16[8,64,320]{2,1,0:T(8,128)(2,1)S(1)}, u32[]{:S(2)}) copy-start(bf16[8,64,320]{2,1,0:T(8,128)(2,1)S(1)} %get-tuple-element.22) | copy-start | bytes 983044
  98.7 5.8 %copy-start.11 = (bf16[8,64,320]{2,1,0:T(8,128)(2,1)}, bf16[8,64,320]{2,1,0:T(8,128)(2,1)S(1)}, u32[]{:S(2)}) copy-start(bf16[8,64,320]{2,1,0:T(8,128)(2,1)S(1)} %get-tuple-element.23) | copy-start | bytes 983044
  98.7 5.8 %copy-start.13 = (bf16[8,64,320]{2,1,0:T(8,128)(2,1)}, bf16[8,64,320]{2,1,0:T(8,128)(2,1)S(1)}, u32[]{:S(2)}) copy-start(bf16[8,64,320]{2,1,0:T(8,128)(2,1)S(1)} %get-tuple-element.24) | copy-start | bytes 983044
  98.7 5.8 %copy-start.10 = (bf16[8,64,320]{2,1,0:T(8,128)(2,1)}, bf16[8,64,320]{2,1,0:T(8,128)(2,1)S(1)}, u32[]{:S(2)}) copy-start(bf16[8,64,320]{2,1,0:T(8,128)(2,1)S(1)} %get-tuple-element.25) | copy-start | bytes 983044
  120.6 7.8 %copy-start.8 = (bf16[8,64,320]{2,1,0:T(8,128)(2,1)S(1)}, bf16[8,64,320]{2,1,0:T(8,128)(2,1)}, u32[]{:S(2)}) copy-start(bf16[8,64,320]{2,1,0:T(8,128)(2,1)} %copy-done.7) | copy-start | bytes 983044
  133.6 51.4 %all-to-all-start.2 = ((bf16[16,32,1800]{2,0,1:T(8,128)(2,1)}), bf16[16,32,1800]{2,0,1:T(8,128)(2,1)}, u32[]{:S(2)}, u32[]{:S(2)}) async-start(bf16[16,32,1800]{2,0,1:T(8,128)(2,1)} %copy.68), calls=%async_computation.2 | async-start | bytes 3932160 | tf_op jit(solution)/shard_map/all_to_all | solution.py:113
  142.6 2.9 %copy-start.18 = (bf16[8,64,320]{2,1,0:T(8,128)(2,1)S(1)}, bf16[8,64,320]{2,1,0:T(8,128)(2,1)}, u32[]{:S(2)}) copy-start(bf16[8,64,320]{2,1,0:T(8,128)(2,1)} %copy-done.17) | copy-start | bytes 983044
  142.6 2.9 %copy-start.23 = (f32[512,320]{0,1:T(8,128)S(1)}, f32[512,320]{0,1:T(8,128)}, u32[]{:S(2)}) copy-start(f32[512,320]{0,1:T(8,128)} %fusion.53) | copy-start | bytes 1966084
  142.6 3.3 %copy-start.14 = (bf16[8,64,320]{2,1,0:T(8,128)(2,1)S(1)}, bf16[8,64,320]{2,1,0:T(8,128)(2,1)}, u32[]{:S(2)}) copy-start(bf16[8,64,320]{2,1,0:T(8,128)(2,1)} %copy-done.13) | copy-start | bytes 983044
  145.5 1.0 copy-start.12
  145.9 1.1 copy-start.21
  145.9 1.3 copy-start.22
  146.5 1.1 copy-start.16
  147.2 1.7 copy-start.3
  147.2 1.7 copy-start.27
  147.6 1.7 copy-start.25
  148.8 1.1 copy-start.24
  149.3 1.1 copy-start.20
  149.8 1.0 copy-start.26
  150.4 1.1 copy-start.28
  150.4 1.2 copy-start.29
  152.8 45.3 %copy-start.6 = (bf16[8,64,320]{2,1,0:T(8,128)(2,1)S(1)}, bf16[8,64,320]{2,1,0:T(8,128)(2,1)}, u32[]{:S(2)}) copy-start(bf16[8,64,320]{2,1,0:T(8,128)(2,1)} %copy-done.5) | copy-start | bytes 983044
  152.8 45.3 %copy-start.19 = (f32[512,320]{0,1:T(8,128)S(1)}, f32[512,320]{0,1:T(8,128)}, u32[]{:S(2)}) copy-start(f32[512,320]{0,1:T(8,128)} %convolution_add_fusion.15) | copy-start | bytes 1966084
  185.0 21.3 %all-to-all-start.1 = ((bf16[16,2,900]{2,1,0:T(2,128)(2,1)}), bf16[16,2,900]{2,1,0:T(2,128)(2,1)S(1)}, u32[]{:S(2)}, u32[]{:S(2)}) async-start(bf16[16,2,900]{2,1,0:T(2,128)(2,1)} %reshape.202), calls=%async_computation.1 | async-start | bytes 131072 | tf_op jit(solution)/shard_map/all_to_all | solution.py:120
  206.2 15.0 %all-to-all-start.3 = ((bf16[16,2,900]{2,1,0:T(2,128)(2,1)}), bf16[16,2,900]{2,1,0:T(2,128)(2,1)S(1)}, u32[]{:S(2)}, u32[]{:S(2)}) async-start(bf16[16,2,900]{2,1,0:T(2,128)(2,1)} %reshape.204), calls=%async_computation.3 | async-start | bytes 131072 | tf_op jit(solution)/shard_map/all_to_all | solution.py:123
where the time goes:
time: 224 us; the launch traced here: 222 us
  starting transfers between devices  75.2 us (34%)
  local copies, waits for them, and re-layouts  49.6 us (22%)
  matrix products  44.8 us (20%)
  waiting for transfers between devices  35.8 us (16%)
  other arithmetic  15.3 us (7%)
    all_to_all x1, waiting for transfers between devices, local(): lax.all_to_all(second_grid.astype(jnp.bfloat16), 'space', split_axis=1, c...  28.3 us
    dot_general x36, matrix products, conv_sum(): lax.dot_general(piece, weight[:, i, j, :], (((1,), (weight_dim,)), ((), (...  24.5 us
    all_to_all x1, starting transfers between devices, local(): lax.all_to_all(first_grid.astype(jnp.bfloat16), 'space', split_axis=1, co...  23.4 us
    ppermute x4, starting transfers between devices, extended(): lax.ppermute(tail, axis, [(i, (i + 1) % count) for i in range(ends)])  17.2 us
    all_to_all x1, starting transfers between devices, local(): lax.all_to_all(summed_first.astype(jnp.bfloat16), 'dp', split_axis=0, con...  13.1 us
    dot_general x9, matrix products, weight_terms(): lax.dot_general(piece, other, (((0,), (0,)), ((), ())), preferred_element...  10.9 us
    dot_general x9, matrix products, weight_terms(): lax.dot_general(other, piece, (((0,), (0,)), ((), ())), preferred_element...  9.41 us
    convert_element_type x2, local copies, waits for them, and re-layouts, local(): second_grid.astype(jnp.bfloat16)  8.98 us
  transfers between devices with their start and end apart: 12, of which 3 were waited for; matrix products, arithmetic and copies ran while one was open for 38% of the time, Pallas kernels for 0%

commit v1 on v0

v1 whole, which is shorter than its diff:
```python
import jax
import jax.numpy as jnp
from jax import lax
from jax.experimental import pallas as pl
from jax.experimental.pallas import tpu as pltpu
from jax.sharding import PartitionSpec as P

BF = jnp.bfloat16
F32 = jnp.float32
MESH = pl.DeviceIdType.MESH
COLS = 64
CH = 320
ROWS = 8
OWN = ROWS * COLS
EXT = (ROWS + 4) * COLS
MID = (ROWS + 2) * COLS
NT = (((1,), (1,)), ((), ()))
UNIT = 360
LANES = 384
UNITS = 40


def dot(a, b):
    return jnp.dot(a, b, preferred_element_type=F32)


def dot_nt(a, b):
    return lax.dot_general(a, b, NT, preferred_element_type=F32)


def column_shifts(value):
    count = value.shape[0]
    col = lax.broadcasted_iota(jnp.int32, value.shape, 0) % COLS
    before = jnp.where(col == 0, 0.0, pltpu.roll(value, 1, 0))
    after = jnp.where(col == COLS - 1, 0.0, pltpu.roll(value, count - 1, 0))
    return before.astype(BF), value.astype(BF), after.astype(BF)


def unit_pieces(u):
    pieces = []
    start, left, lane = UNIT * u, UNIT, 0
    while left:
        tap, col = divmod(start, 3 * CH)
        size = min(left, 3 * CH - col)
        pieces.append((tap, col, size, lane))
        start, left, lane = start + size, left - size, lane + size
    return pieces


def kernel(
    lat_hbm, w1_hbm, w2_hbm, cot_hbm, out_hbm, lg_hbm, g1_ref, g2_ref,
    latx, cotx, act, a3, c3, w1, w2, w1t, w2t, acc, slope, h3, hg3, terms, perm, lhs_t,
    grid, core_recv, zsum, zrecv, xs, xf, xr, sc, ys, yr, outv, lgv,
    load_sem, halo_send, halo_recv, core_send, core_rsem, zsend, zrsem, xsend, xrsem, ysend, yrsem, store_sem,
):
    dp, space = lax.axis_index("dp"), lax.axis_index("space")
    yy, core = dp // 2, dp % 2
    zz, xx = space // 4, space % 4
    up, down = (space + 31) % 32, (space + 1) % 32

    loads = [
        pltpu.make_async_copy(lat_hbm, latx.at[pl.ds(2 * COLS, OWN)], load_sem.at[0]),
        pltpu.make_async_copy(cot_hbm, cotx.at[pl.ds(2 * COLS, OWN)], load_sem.at[1]),
        pltpu.make_async_copy(w1_hbm, w1, load_sem.at[2]),
        pltpu.make_async_copy(w2_hbm, w2, load_sem.at[3]),
    ]
    for load in loads:
        load.start()

    peers = [(dp, up), (dp, down), (yy * 2 + 1 - core, space)]
    peers += [(dp, (zz + k) % 8 * 4 + xx) for k in (1, 7)]
    peers += [(dp, zz * 4 + (xx + k) % 4) for k in (1, 2, 3)]
    peers += [((yy + k) % 8 * 2 + core, space) for k in range(1, 8)]
    barrier = pltpu.get_barrier_semaphore()
    for peer in peers:
        pl.semaphore_signal(barrier, inc=1, device_id=peer, device_id_type=MESH)

    def widen(src, dst, first, last, flip, activate):
        def group(k, _):
            at = pl.ds(pl.multiple_of(k * COLS, COLS), COLS)
            value = src[at, :].astype(F32)
            if activate:
                value = value * jax.nn.sigmoid(value)
                act[at, :] = value.astype(BF)
            one, two, three = column_shifts(value)
            dst[at, :] = jnp.concatenate([three, two, one] if flip else [one, two, three], axis=1)
            return 0
        lax.fori_loop(first, last, group, 0)

    loads[0].wait()
    widen(latx, a3, 2, 10, False, True)
    loads[1].wait()
    widen(cotx, c3, 2, 10, True, False)

    pl.semaphore_wait(barrier, len(peers))
    halos = []
    for n, (src, dst) in enumerate(((lat_hbm, latx), (cot_hbm, cotx))):
        to_up = pltpu.make_async_remote_copy(
            src_ref=src.at[pl.ds(0, 2 * COLS)], dst_ref=dst.at[pl.ds(10 * COLS, 2 * COLS)],
            send_sem=halo_send.at[2 * n], recv_sem=halo_recv.at[2 * n],
            device_id=(dp, up), device_id_type=MESH)
        to_down = pltpu.make_async_remote_copy(
            src_ref=src.at[pl.ds(6 * COLS, 2 * COLS)], dst_ref=dst.at[pl.ds(0, 2 * COLS)],
            send_sem=halo_send.at[2 * n + 1], recv_sem=halo_recv.at[2 * n + 1],
            device_id=(dp, down), device_id_type=MESH)
        halos.append((to_up, to_down))

    @pl.when(space > 0)
    def _():
        for to_up, _d in halos:
            to_up.start()

    @pl.when(space < 31)
    def _():
        for _u, to_down in halos:
            to_down.start()

    shape = (CH, CH)
    row = lax.broadcasted_iota(jnp.int32, shape, 0)
    chan = lax.broadcasted_iota(jnp.int32, shape, 1)
    group = ((row % 8) * 2 + row // 32 % 2) * 4 + row // 8 % 4
    perm[...] = jnp.where(chan == 5 * group + row // 64, 1.0, 0.0).astype(BF)
    lhs_t[...] = dot_nt(perm[...], cotx[2 * COLS : 10 * COLS, :]).astype(BF)

    loads[2].wait()

    def conv_one(first, count):
        size = count * COLS
        total = dot(a3[first * COLS : first * COLS + size, :], w1[0])
        total += dot(a3[(first + 1) * COLS : (first + 1) * COLS + size, :], w1[1])
        total += dot(a3[(first + 2) * COLS : (first + 2) * COLS + size, :], w1[2])
        acc[first * COLS : first * COLS + size, :] = total

        def finish(k, _):
            at = pl.ds(pl.multiple_of(k * COLS, COLS), COLS)
            hidden = acc[at, :].astype(BF).astype(F32)
            sig = jax.nn.sigmoid(hidden)
            slope[at, :] = sig * (1.0 + hidden * (1.0 - sig))
            h3[at, :] = jnp.concatenate(column_shifts(hidden * sig), axis=1)
            return 0

        lax.fori_loop(first, first + count, finish, 0)

    conv_one(2, 6)

    @pl.when(space == 0)
    def _():
        latx[0 : 2 * COLS, :] = jnp.zeros((2 * COLS, CH), BF)
        cotx[0 : 2 * COLS, :] = jnp.zeros((2 * COLS, CH), BF)

    @pl.when(space == 31)
    def _():
        latx[10 * COLS :, :] = jnp.zeros((2 * COLS, CH), BF)
        cotx[10 * COLS :, :] = jnp.zeros((2 * COLS, CH), BF)

    @pl.when(space < 31)
    def _():
        for to_up, _d in halos:
            to_up.wait_recv()

    @pl.when(space > 0)
    def _():
        for _u, to_down in halos:
            to_down.wait_recv()

    for first in (0, 10):
        widen(latx, a3, first, first + 2, False, True)
        widen(cotx, c3, first, first + 2, True, False)
    conv_one(0, 2)
    conv_one(8, 2)

    def clear_outside(ref):
        @pl.when(space == 0)
        def _():
            ref[0:COLS, :] = jnp.zeros((COLS, 3 * CH), BF)

        @pl.when(space == 31)
        def _():
            ref[9 * COLS :, :] = jnp.zeros((COLS, 3 * CH), BF)

    clear_outside(h3)

    other = (yy * 2 + 1 - core, space)

    def core_copy(n, r):
        return pltpu.make_async_remote_copy(
            src_ref=grid.at[n, pl.ds(8 * r, 8), pl.ds(4 * (1 - core), 4)],
            dst_ref=core_recv.at[n, pl.ds(8 * r, 8)],
            send_sem=core_send.at[n, r], recv_sem=core_rsem.at[n, r],
            device_id=other, device_id_type=MESH)

    def pack_terms(n):
        lane = lax.broadcasted_iota(jnp.int32, (64, LANES), 1)
        for r in range(5):
            for u in range(8):
                value = None
                for tap, col, size, put in unit_pieces(u):
                    base = min(col // 128 * 128, 1024 - LANES)
                    width = -(-max(col - base + size, LANES) // 128) * 128
                    shift = (put - (col - base)) % width
                    piece = terms[tap, 64 * r : 64 * r + 64, base : base + width]
                    if shift:
                        piece = pltpu.roll(piece, shift, 1)
                    piece = piece[:, :LANES]
                    value = piece if value is None else jnp.where(lane < put, value, piece)
                grid[n, 8 * r + u] = value.reshape(8, 8, LANES).astype(BF)
            core_copy(n, r).start()

    def core_sum(n):
        for r in range(5):
            core_copy(n, r).wait_recv()
            for k in range(4):
                zsum[n, k, 8 * r : 8 * r + 8] = (
                    grid[n, 8 * r : 8 * r + 8, 4 * core + k].astype(F32)
                    + core_recv[n, 8 * r : 8 * r + 8, k].astype(F32)
                ).astype(BF)

    def block(n, target, lo, size):
        return zsum.at[n, target // 2, pl.ds(20 * (target % 2) + lo, size)]

    def zcopy(n, s, way):
        step = 1 if way == 0 else 7
        target = (zz + step * (5 - s)) % 8
        lo, size = (10 * way, 10) if s == 1 else (0, 20)
        return pltpu.make_async_remote_copy(
            src_ref=block(n, target, lo, size),
            dst_ref=zrecv.at[n, way, s - 1, pl.ds(lo, size)],
            send_sem=zsend.at[n, way, s - 1], recv_sem=zrsem.at[n, way, s - 1],
            device_id=(dp, (zz + step) % 8 * 4 + xx), device_id_type=MESH)

    def zstep(n, s):
        for way in range(2):
            if s >= 2:
                zcopy(n, s - 1, way).wait_recv()
                step = 1 if way == 0 else 7
                target = (zz + step * (5 - s)) % 8
                lo, size = (10 * way, 10) if s == 2 else (0, 20)
                ref = block(n, target, lo, size)
                got = zrecv[n, way, s - 2, lo : lo + size]
                ref[...] = (ref[...].astype(F32) + got.astype(F32)).astype(BF)
            zcopy(n, s, way).start()

    def xcopy(n, d):
        to = (xx + d) % 4
        return pltpu.make_async_remote_copy(
            src_ref=xs.at[n, pl.ds(5 * to, 5)], dst_ref=xr.at[n, d - 1],
            send_sem=xsend.at[n, d - 1], recv_sem=xrsem.at[n, d - 1],
            device_id=(dp, zz * 4 + to), device_id_type=MESH)

    def zfinal(n):
        for way in range(2):
            zcopy(n, 4, way).wait_recv()
        total = block(n, zz, 0, 20)[...].astype(F32) + zrecv[n, 0, 3].astype(F32) + zrecv[n, 1, 3].astype(F32)
        xf[n] = total
        xs[n] = total.astype(BF)
        for d in (1, 2, 3):
            xcopy(n, d).start()

    def ycopy(n, d):
        to = (yy + d) % 8
        return pltpu.make_async_remote_copy(
            src_ref=ys.at[n, to], dst_ref=yr.at[n, d - 1],
            send_sem=ysend.at[n, d - 1], recv_sem=yrsem.at[n, d - 1],
            device_id=(to * 2 + core, space), device_id_type=MESH)

    def xfinal(n):
        total = xf[n, pl.ds(5 * xx, 5)]
        for d in (1, 2, 3):
            xcopy(n, d).wait_recv()
            total += xr[n, d - 1].astype(F32)
        flat = total.reshape(5 * 8, LANES)
        for k in range(3):
            sc[n, k] = flat[:, 128 * k : 128 * k + 128]
        for to in range(8):
            for k in range(3):
                ys[n, to, 0:5, 128 * k : 128 * k + 128] = sc[n, k, pl.ds(to, 5, stride=8), :].astype(BF)
        for d in range(1, 8):
            ycopy(n, d).start()

    def yfinal(n, ref):
        total = ys[n, yy].astype(F32)
        for d in range(1, 8):
            ycopy(n, d).wait_recv()
            total += yr[n, d - 1].astype(F32)
        ref[...] = total

    ys[...] = jnp.zeros(ys.shape, BF)
    for i in range(3):
        terms[i, :, 3 * CH :] = jnp.zeros((CH, 64), F32)

    for i in range(3):
        terms[i, :, : 3 * CH] = dot(lhs_t[...], h3[i * COLS : i * COLS + OWN, :])
    pack_terms(1)

    loads[3].wait()
    total = dot(c3[2 * COLS : 2 * COLS + MID, :], w2[0])
    total += dot(c3[COLS : COLS + MID, :], w2[1])
    total += dot(c3[0:MID, :], w2[2])
    acc[...] = total

    def finish_back(k, _):
        at = pl.ds(pl.multiple_of(k * COLS, COLS), COLS)
        before, here, after = column_shifts(acc[at, :] * slope[at, :])
        hg3[at, :] = jnp.concatenate([after, here, before], axis=1)
        return 0

    lax.fori_loop(0, 10, finish_back, 0)
    clear_outside(hg3)

    core_sum(1)
    zstep(1, 1)

    for i in range(3):
        left = dot_nt(perm[...], act[(i + 1) * COLS : (i + 1) * COLS + OWN, :]).astype(BF)
        terms[i, :, : 3 * CH] = dot(left, hg3[COLS : COLS + OWN, :])
    zstep(1, 2)
    pack_terms(0)
    zstep(1, 3)

    for i in range(3):
        w2t[i] = jnp.concatenate([w2[i, CH * j : CH * j + CH, :] for j in range(3)], axis=1)
        w1t[i] = jnp.concatenate([w1[i, CH * j : CH * j + CH, :] for j in range(3)], axis=1)
    core_sum(0)
    zstep(0, 1)
    zstep(1, 4)

    total = dot_nt(h3[0:OWN, :], w2t[0])
    total += dot_nt(h3[COLS : COLS + OWN, :], w2t[1])
    total += dot_nt(h3[2 * COLS : 2 * COLS + OWN, :], w2t[2])
    outv[...] = total.astype(BF)
    store_out = pltpu.make_async_copy(outv, out_hbm, store_sem.at[0])
    store_out.start()
    zstep(0, 2)
    zfinal(1)

    total = dot_nt(hg3[2 * COLS : 2 * COLS + OWN, :], w1t[0])
    total += dot_nt(hg3[COLS : COLS + OWN, :], w1t[1])
    total += dot_nt(hg3[0:OWN, :], w1t[2])
    acc[0:OWN, :] = total
    zstep(0, 3)

    def finish_latent(k, _):
        at = pl.ds(pl.multiple_of(k * COLS, COLS), COLS)
        value = latx[pl.ds(pl.multiple_of((k + 2) * COLS, COLS), COLS), :].astype(F32)
        sig = jax.nn.sigmoid(value)
        lgv[at, :] = (acc[at, :] * (sig * (1.0 + value * (1.0 - sig)))).astype(BF)
        return 0

    lax.fori_loop(0, 8, finish_latent, 0)
    store_lg = pltpu.make_async_copy(lgv, lg_hbm, store_sem.at[1])
    store_lg.start()
    xfinal(1)
    zstep(0, 4)
    yfinal(1, g2_ref)
    zfinal(0)
    xfinal(0)
    yfinal(0, g1_ref)

    @pl.when(space > 0)
    def _():
        for to_up, _d in halos:
            to_up.wait_send()

    @pl.when(space < 31)
    def _():
        for _u, to_down in halos:
            to_down.wait_send()

    for n in range(2):
        for r in range(5):
            core_copy(n, r).wait_send()
        for s in range(1, 5):
            for way in range(2):
                zcopy(n, s, way).wait_send()
        for d in (1, 2, 3):
            xcopy(n, d).wait_send()
        for d in range(1, 8):
            ycopy(n, d).wait_send()
    store_out.wait()
    store_lg.wait()


def local(latent, first_weight, second_weight, cotangent):
    def taps(weight):
        return jnp.transpose(weight, (1, 2, 0, 3)).reshape(3, 3 * CH, CH)

    any_spec = pl.BlockSpec(memory_space=pl.ANY)
    vmem_spec = pl.BlockSpec(memory_space=pltpu.VMEM)
    dma = pltpu.SemaphoreType.DMA
    out, latent_grad, first, second = pl.pallas_call(
        kernel,
        out_shape=(
            jax.ShapeDtypeStruct((OWN, CH), BF),
            jax.ShapeDtypeStruct((OWN, CH), BF),
            jax.ShapeDtypeStruct((8, LANES), F32),
            jax.ShapeDtypeStruct((8, LANES), F32),
        ),
        in_specs=[any_spec] * 4,
        out_specs=(any_spec, any_spec, vmem_spec, vmem_spec),
        scratch_shapes=[
            pltpu.VMEM((EXT, CH), BF),
            pltpu.VMEM((EXT, CH), BF),
            pltpu.VMEM((EXT, CH), BF),
            pltpu.VMEM((EXT, 3 * CH), BF),
            pltpu.VMEM((EXT, 3 * CH), BF),
            pltpu.VMEM((3, 3 * CH, CH), BF),
            pltpu.VMEM((3, 3 * CH, CH), BF),
            pltpu.VMEM((3, CH, 3 * CH), BF),
            pltpu.VMEM((3, CH, 3 * CH), BF),
            pltpu.VMEM((MID, CH), F32),
            pltpu.VMEM((MID, CH), F32),
            pltpu.VMEM((MID, 3 * CH), BF),
            pltpu.VMEM((MID, 3 * CH), BF),
            pltpu.VMEM((3, CH, 1024), F32),
            pltpu.VMEM((CH, CH), BF),
            pltpu.VMEM((CH, OWN), BF),
            pltpu.VMEM((2, UNITS, 8, 8, LANES), BF),
            pltpu.VMEM((2, UNITS, 4, 8, LANES), BF),
            pltpu.VMEM((2, 4, UNITS, 8, LANES), BF),
            pltpu.VMEM((2, 2, 4, 20, 8, LANES), BF),
            pltpu.VMEM((2, 20, 8, LANES), BF),
            pltpu.VMEM((2, 20, 8, LANES), F32),
            pltpu.VMEM((2, 3, 5, 8, LANES), BF),
            pltpu.VMEM((2, 3, 40, 128), F32),
            pltpu.VMEM((2, 8, 8, LANES), BF),
            pltpu.VMEM((2, 7, 8, LANES), BF),
            pltpu.VMEM((OWN, CH), BF),
            pltpu.VMEM((OWN, CH), BF),
            dma((4,)),
            dma((4,)),
            dma((4,)),
            dma((2, 5)),
            dma((2, 5)),
            dma((2, 2, 4)),
            dma((2, 2, 4)),
            dma((2, 3)),
            dma((2, 3)),
            dma((2, 7)),
            dma((2, 7)),
            dma((2,)),
        ],
        compiler_params=pltpu.CompilerParams(
            collective_id=0, has_side_effects=True, vmem_limit_bytes=60 * 1024 * 1024
        ),
        name="conv_pair",
    )(
        latent.reshape(OWN, CH), taps(first_weight), taps(second_weight), cotangent.reshape(OWN, CH)
    )
    return (
        out.reshape(1, ROWS, COLS, CH),
        latent_grad.reshape(1, ROWS, COLS, CH),
        first[:5, :UNIT].reshape(-1),
        second[:5, :UNIT].reshape(-1),
    )


def solution(mesh):
    placed = (P("dp", "space", None, None), P(), P(), P("dp", "space", None, None))
    return jax.shard_map(
        local,
        mesh=mesh,
        in_specs=placed,
        out_specs=(
            P("dp", "space", None, None),
            P("dp", "space", None, None),
            P(("dp", "space")),
            P(("dp", "space")),
        ),
        check_vma=False,
    )
```

time: 224 us -> 75.6 us (0.34)
  the two profiles are of different devices: /device:TPU:1 before, /device:TPU:2 now
where the time goes in v1:
time: 75.6 us; the launch traced here: 75.3 us
  Pallas kernels  68.4 us (90%)
  local copies, waits for them, and re-layouts  6.32 us (8%)
    pallas_call x1, Pallas kernels, local(): pl.pallas_call(kernel, out_shape=(jax.ShapeDtypeStruct((OWN, CH), BF), ja...  68.4 us
    unnamed x2, local copies, waits for them, and re-layouts  3.56 us

profile of v1, /device:TPU:2, one launch (start us, length us, event | category | flops | bytes accessed | tf_op | source)
XLA Modules:
  0.0 75.3 jit_solution(4531334702801696753)
XLA Ops:
  0.6 68.4 %conv_pair.1 = (bf16[512,320]{1,0:T(8,128)(2,1)}, bf16[512,320]{1,0:T(8,128)(2,1)}, f32[8,384]{1,0:T(8,128)}, f32[8,384]{1,0:T(8,128)}) custom-call(bf16[512,320]{1,0:T(8,128)(2,1)} %bitcast.14, bf16[3,960,320]{2,1,0:T(8,128)(2,1)} %bitcast.12, bf16[3,960,320]{2,1,0:T(8,128)(2,1)} %bitcast.13, bf16[512,320]{1,0:T(8,128)(2,1)} %bitcast.15), custom_call_target="tpu_custom_call" | custom-call | tf_op jit(solution)/shard_map/conv_pair/pallas_call | solution.py:390
  69.0 1.4 %reshape.38 = f32[1800]{0:T(1024)} reshape(f32[5,360]{1,0:T(8,128)} %bitcast.19) | data formatting | bytes 14400 | tf_op jit(solution)/shard_map/reshape | solution.py:452
  70.4 1.4 %reshape.39 = f32[1800]{0:T(1024)} reshape(f32[5,360]{1,0:T(8,128)} %bitcast.18) | data formatting | bytes 14400 | tf_op jit(solution)/shard_map/reshape | solution.py:453
  71.8 1.8 %copy.10 = bf16[1,8,64,320]{3,2,1,0:T(8,128)(2,1)} copy(bf16[1,8,64,320]{3,2,1,0:T(8,128)(2,1)} %bitcast.17) | data formatting | bytes 655360
  73.6 1.8 %copy.11 = bf16[1,8,64,320]{3,2,1,0:T(8,128)(2,1)} copy(bf16[1,8,64,320]{3,2,1,0:T(8,128)(2,1)} %bitcast.16) | data formatting | bytes 655360

commit v2 on v1

--- a/solution.py
+++ b/solution.py
@@ -50,8 +50,8 @@
 def kernel(
     lat_hbm, w1_hbm, w2_hbm, cot_hbm, out_hbm, lg_hbm, g1_ref, g2_ref,
     latx, cotx, act, a3, c3, w1, w2, w1t, w2t, acc, slope, h3, hg3, terms, perm, lhs_t,
-    grid, core_recv, zsum, zrecv, xs, xf, xr, sc, ys, yr, outv, lgv,
-    load_sem, halo_send, halo_recv, core_send, core_rsem, zsend, zrsem, xsend, xrsem, ysend, yrsem, store_sem,
+    grid, core_recv, sums, zrecv, xrecv, late, mids, midr, sc, ys, yr, outv, lgv,
+    load_sem, halo_send, halo_recv, core_send, core_rsem, zsend, zrsem, lsend, lrsem, ysend, yrsem, store_sem,
 ):
     dp, space = lax.axis_index("dp"), lax.axis_index("space")
     yy, core = dp // 2, dp % 2
@@ -68,7 +68,7 @@
         load.start()
 
     peers = [(dp, up), (dp, down), (yy * 2 + 1 - core, space)]
-    peers += [(dp, (zz + k) % 8 * 4 + xx) for k in (1, 7)]
+    peers += [(dp, (zz + k) % 8 * 4 + xx) for k in range(1, 8)]
     peers += [(dp, zz * 4 + (xx + k) % 4) for k in (1, 2, 3)]
     peers += [((yy + k) % 8 * 2 + core, space) for k in range(1, 8)]
     barrier = pltpu.get_barrier_semaphore()
@@ -209,80 +209,161 @@
     def core_sum(n):
         for r in range(5):
             core_copy(n, r).wait_recv()
-            for k in range(4):
-                zsum[n, k, 8 * r : 8 * r + 8] = (
-                    grid[n, 8 * r : 8 * r + 8, 4 * core + k].astype(F32)
-                    + core_recv[n, 8 * r : 8 * r + 8, k].astype(F32)
-                ).astype(BF)
-
-    def block(n, target, lo, size):
-        return zsum.at[n, target // 2, pl.ds(20 * (target % 2) + lo, size)]
+        for k in range(4):
+            part = grid[n, :, 4 * core + k].astype(F32) + core_recv[n, :, k].astype(F32)
+            sums[n, k] = part.reshape(2, 4, 5, 8, LANES).astype(BF)
+
+    steps = (1, 7)
+
+    def zblock(ref, n, target, way, half):
+        lo, size = (2 * way, 2) if half else (0, 4)
+        return ref.at[n, target // 2, target % 2, pl.ds(lo, size)]
 
     def zcopy(n, s, way):
-        step = 1 if way == 0 else 7
-        target = (zz + step * (5 - s)) % 8
-        lo, size = (10 * way, 10) if s == 1 else (0, 20)
+        target = (zz + steps[way] * (5 - s)) % 8
+        lo, size = (2 * way, 2) if s == 1 else (0, 4)
         return pltpu.make_async_remote_copy(
-            src_ref=block(n, target, lo, size),
+            src_ref=zblock(sums, n, target, way, s == 1),
             dst_ref=zrecv.at[n, way, s - 1, pl.ds(lo, size)],
             send_sem=zsend.at[n, way, s - 1], recv_sem=zrsem.at[n, way, s - 1],
-            device_id=(dp, (zz + step) % 8 * 4 + xx), device_id_type=MESH)
+            device_id=(dp, (zz + steps[way]) % 8 * 4 + xx), device_id_type=MESH)
 
     def zstep(n, s):
         for way in range(2):
             if s >= 2:
                 zcopy(n, s - 1, way).wait_recv()
-                step = 1 if way == 0 else 7
-                target = (zz + step * (5 - s)) % 8
-                lo, size = (10 * way, 10) if s == 2 else (0, 20)
-                ref = block(n, target, lo, size)
-                got = zrecv[n, way, s - 2, lo : lo + size]
-                ref[...] = (ref[...].astype(F32) + got.astype(F32)).astype(BF)
+                ref = zblock(sums, n, (zz + steps[way] * (5 - s)) % 8, way, s == 2)
+                lo, size = (2 * way, 2) if s == 2 else (0, 4)
+                ref[...] = (ref[...].astype(F32) + zrecv[n, way, s - 2, lo : lo + size].astype(F32)).astype(BF)
             zcopy(n, s, way).start()
 
-    def xcopy(n, d):
+    def xcopy(n, s, way):
+        target = (xx + (1 if way == 0 else 3) * (3 - s)) % 4
+        lo, size = (2 * way, 2) if s == 1 else (0, 4)
+        return pltpu.make_async_remote_copy(
+            src_ref=sums.at[n, pl.ds(lo, size), :, target],
+            dst_ref=xrecv.at[n, way, s - 1, pl.ds(lo, size)],
+            send_sem=zsend.at[n, way, s - 1], recv_sem=zrsem.at[n, way, s - 1],
+            device_id=(dp, zz * 4 + (xx + (1 if way == 0 else 3)) % 4), device_id_type=MESH)
+
+    def xstep(n, s):
+        for way in range(2):
+            if s == 2:
+                xcopy(n, 1, way).wait_recv()
+                lo = 2 * way
+                ref = sums.at[n, pl.ds(lo, 2), :, (xx + (1 if way == 0 else 3)) % 4]
+                ref[...] = (ref[...].astype(F32) + xrecv[n, way, 0, lo : lo + 2].astype(F32)).astype(BF)
+            xcopy(n, s, way).start()
+
+    def x_direct(n, d):
         to = (xx + d) % 4
         return pltpu.make_async_remote_copy(
-            src_ref=xs.at[n, pl.ds(5 * to, 5)], dst_ref=xr.at[n, d - 1],
-            send_sem=xsend.at[n, d - 1], recv_sem=xrsem.at[n, d - 1],
+            src_ref=sums.at[n, zz // 2, zz % 2, to], dst_ref=late.at[n, d - 1],
+            send_sem=lsend.at[n, d - 1], recv_sem=lrsem.at[n, d - 1],
             device_id=(dp, zz * 4 + to), device_id_type=MESH)
+
+    def y_direct(n, d):
+        to = (yy + d) % 8
+        return pltpu.make_async_remote_copy(
+            src_ref=mids.at[n, to], dst_ref=midr.at[n, d - 1],
+            send_sem=lsend.at[n, d - 1], recv_sem=lrsem.at[n, d - 1],
+            device_id=(to * 2 + core, space), device_id_type=MESH)
 
     def zfinal(n):
         for way in range(2):
             zcopy(n, 4, way).wait_recv()
-        total = block(n, zz, 0, 20)[...].astype(F32) + zrecv[n, 0, 3].astype(F32) + zrecv[n, 1, 3].astype(F32)
-        xf[n] = total
-        xs[n] = total.astype(BF)
-        for d in (1, 2, 3):
-            xcopy(n, d).start()
-
-    def ycopy(n, d):
-        to = (yy + d) % 8
+        ref = sums.at[n, zz // 2, zz % 2]
+        ref[...] = (ref[...].astype(F32) + zrecv[n, 0, 3].astype(F32) + zrecv[n, 1, 3].astype(F32)).astype(BF)
+        for d in range(1, 4):
+            x_direct(n, d).start()
+
+    def xfinal(n):
+        for way in range(2):
+            xcopy(n, 2, way).wait_recv()
+        total = sums[n, :, :, xx].astype(F32) + xrecv[n, 0, 1].astype(F32) + xrecv[n, 1, 1].astype(F32)
+        flat = total.reshape(40 * 8, LANES)
+        for k in range(3):
+            sc[k] = flat[:, 128 * k : 128 * k + 128]
+        for to in range(8):
+            for k in range(3):
+                mids[n, to, :, 128 * k : 128 * k + 128] = sc[k, pl.ds(to, 40, stride=8), :].astype(BF)
+        for d in range(1, 8):
+            y_direct(n, d).start()
+
+    def last_copy(n, d, over_y):
+        if over_y:
+            to = (yy + d) % 8
+            device = (to * 2 + core, space)
+        else:
+            to = (zz + d) % 8
+            device = (dp, to * 4 + xx)
         return pltpu.make_async_remote_copy(
             src_ref=ys.at[n, to], dst_ref=yr.at[n, d - 1],
             send_sem=ysend.at[n, d - 1], recv_sem=yrsem.at[n, d - 1],
-            device_id=(to * 2 + core, space), device_id_type=MESH)
-
-    def xfinal(n):
-        total = xf[n, pl.ds(5 * xx, 5)]
-        for d in (1, 2, 3):
-            xcopy(n, d).wait_recv()
-            total += xr[n, d - 1].astype(F32)
+            device_id=device, device_id_type=MESH)
+
+    def x_finish(n):
+        total = sums[n, zz // 2, zz % 2, xx].astype(F32)
+        for d in range(1, 4):
+            x_direct(n, d).wait_recv()
+            total += late[n, d - 1].astype(F32)
         flat = total.reshape(5 * 8, LANES)
         for k in range(3):
-            sc[n, k] = flat[:, 128 * k : 128 * k + 128]
+            sc[k, 0:40] = flat[:, 128 * k : 128 * k + 128]
         for to in range(8):
             for k in range(3):
-                ys[n, to, 0:5, 128 * k : 128 * k + 128] = sc[n, k, pl.ds(to, 5, stride=8), :].astype(BF)
+                ys[n, to, 0:5, 128 * k : 128 * k + 128] = sc[k, pl.ds(to, 5, stride=8), :].astype(BF)
         for d in range(1, 8):
-            ycopy(n, d).start()
-
-    def yfinal(n, ref):
-        total = ys[n, yy].astype(F32)
+            last_copy(n, d, True).start()
+
+    def y_finish(n):
+        total = mids[n, yy].astype(F32)
         for d in range(1, 8):
-            ycopy(n, d).wait_recv()
-            total += yr[n, d - 1].astype(F32)
-        ref[...] = total
+            y_direct(n, d).wait_recv()
+            total += midr[n, d - 1].astype(F32)
+        for k in range(3):
+            sc[k, 0:40] = total[:, 128 * k : 128 * k + 128]
+        for to in range(8):
+            for k in range(3):
+                ys[n, to, 0:5, 128 * k : 128 * k + 128] = sc[k, 5 * to : 5 * to + 5, :].astype(BF)
+        for d in range(1, 8):
+            last_copy(n, d, False).start()
+
+    def last(n, ref):
+        def total_over(over_y):
+            total = ys[n, yy if over_y else zz].astype(F32)
+            for d in range(1, 8):
+                last_copy(n, d, over_y).wait_recv()
+                total += yr[n, d - 1].astype(F32)
+            ref[...] = total
+
+        @pl.when(core == 0)
+        def _():
+            total_over(True)
+
+        @pl.when(core == 1)
+        def _():
+            total_over(False)
+
+    def advance(n, step):
+        @pl.when(core == 0)
+        def _():
+            if step <= 4:
+                zstep(n, step)
+            elif step == 5:
+                zfinal(n)
+            else:
+                x_finish(n)
+
+        if step in (1, 2, 3, 5):
+            @pl.when(core == 1)
+            def _():
+                if step <= 2:
+                    xstep(n, step)
+                elif step == 3:
+                    xfinal(n)
+                else:
+                    y_finish(n)
 
     ys[...] = jnp.zeros(ys.shape, BF)
     for i in range(3):
@@ -308,21 +389,20 @@
     clear_outside(hg3)
 
     core_sum(1)
-    zstep(1, 1)
+    advance(1, 1)
 
     for i in range(3):
         left = dot_nt(perm[...], act[(i + 1) * COLS : (i + 1) * COLS + OWN, :]).astype(BF)
         terms[i, :, : 3 * CH] = dot(left, hg3[COLS : COLS + OWN, :])
-    zstep(1, 2)
     pack_terms(0)
-    zstep(1, 3)
+    advance(1, 2)
 
     for i in range(3):
         w2t[i] = jnp.concatenate([w2[i, CH * j : CH * j + CH, :] for j in range(3)], axis=1)
         w1t[i] = jnp.concatenate([w1[i, CH * j : CH * j + CH, :] for j in range(3)], axis=1)
     core_sum(0)
-    zstep(0, 1)
-    zstep(1, 4)
+    advance(0, 1)
+    advance(1, 3)
 
     total = dot_nt(h3[0:OWN, :], w2t[0])
     total += dot_nt(h3[COLS : COLS + OWN, :], w2t[1])
@@ -330,14 +410,15 @@
     outv[...] = total.astype(BF)
     store_out = pltpu.make_async_copy(outv, out_hbm, store_sem.at[0])
     store_out.start()
-    zstep(0, 2)
-    zfinal(1)
+    advance(0, 2)
+    advance(1, 4)
 
     total = dot_nt(hg3[2 * COLS : 2 * COLS + OWN, :], w1t[0])
     total += dot_nt(hg3[COLS : COLS + OWN, :], w1t[1])
     total += dot_nt(hg3[0:OWN, :], w1t[2])
     acc[0:OWN, :] = total
-    zstep(0, 3)
+    advance(0, 3)
+    advance(1, 5)
 
     def finish_latent(k, _):
         at = pl.ds(pl.multiple_of(k * COLS, COLS), COLS)
@@ -349,12 +430,12 @@
     lax.fori_loop(0, 8, finish_latent, 0)
     store_lg = pltpu.make_async_copy(lgv, lg_hbm, store_sem.at[1])
     store_lg.start()
-    xfinal(1)
-    zstep(0, 4)
-    yfinal(1, g2_ref)
-    zfinal(0)
-    xfinal(0)
-    yfinal(0, g1_ref)
+    advance(0, 4)
+    advance(1, 6)
+    advance(0, 5)
+    advance(0, 6)
+    last(1, g2_ref)
+    last(0, g1_ref)
 
     @pl.when(space > 0)
     def _():
@@ -369,15 +450,62 @@
     for n in range(2):
         for r in range(5):
             core_copy(n, r).wait_send()
-        for s in range(1, 5):
+
+    @pl.when(core == 0)
+    def _():
+        for n in range(2):
             for way in range(2):
-                zcopy(n, s, way).wait_send()
-        for d in (1, 2, 3):
-            xcopy(n, d).wait_send()
-        for d in range(1, 8):
-            ycopy(n, d).wait_send()
+                for s in range(1, 5):
+                    zcopy(n, s, way).wait_send()
+            for d in range(1, 4):
+                x_direct(n, d).wait_send()
+            for d in range(1, 8):
+                last_copy(n, d, True).wait_send()
+
+    @pl.when(core == 1)
+    def _():
+        for n in range(2):
+            for way in range(2):
+                for s in range(1, 3):
+                    xcopy(n, s, way).wait_send()
+            for d in range(1, 8):
+                y_direct(n, d).wait_send()
+                last_copy(n, d, False).wait_send()
+
     store_out.wait()
     store_lg.wait()
+
+
+def finish_kernel(out_hbm, lg_hbm, g1_ref, g2_ref, out_res, lg_res, f1_ref, f2_ref, buf, sem_in, sem_out):
+    takes, puts = [], []
+    for n, (src, dst) in enumerate(((out_hbm, out_res), (lg_hbm, lg_res))):
+        for k in range(2):
+            at = pl.ds(k * OWN // 2, OWN // 2)
+            takes.append(pltpu.make_async_copy(src.at[at], buf.at[n, at], sem_in.at[n, k]))
+            puts.append(pltpu.make_async_copy(buf.at[n, at], dst.at[at], sem_out.at[n, k]))
+    for take in takes:
+        take.start()
+    for take, put in zip(takes, puts):
+        take.wait()
+        put.start()
+    lane = lax.broadcasted_iota(jnp.int32, (1, 128), 1)
+    for src, dst in ((g1_ref, f1_ref), (g2_ref, f2_ref)):
+        for k in range(15):
+            start, end = 128 * k, min(128 * k + 128, 5 * UNIT)
+            size, value, at = end - start, None, start
+            while at < end:
+                row, col = divmod(at, UNIT)
+                base = min(col // 128 * 128, LANES - 256)
+                piece = src[row : row + 1, base : base + 256]
+                shift = (at - start - (col - base)) % 256
+                if shift:
+                    piece = pltpu.roll(piece, shift, 1)
+                piece = piece[:, :128]
+                value = piece if value is None else jnp.where(lane < at - start, value, piece)
+                at += min(UNIT - col, end - at)
+            dst[pl.ds(start, size)] = value[0, :size]
+    for put in puts:
+        put.wait()
 
 
 def local(latent, first_weight, second_weight, cotangent):
@@ -416,12 +544,13 @@
             pltpu.VMEM((CH, OWN), BF),
             pltpu.VMEM((2, UNITS, 8, 8, LANES), BF),
             pltpu.VMEM((2, UNITS, 4, 8, LANES), BF),
-            pltpu.VMEM((2, 4, UNITS, 8, LANES), BF),
-            pltpu.VMEM((2, 2, 4, 20, 8, LANES), BF),
-            pltpu.VMEM((2, 20, 8, LANES), BF),
-            pltpu.VMEM((2, 20, 8, LANES), F32),
+            pltpu.VMEM((2, 4, 2, 4, 5, 8, LANES), BF),
+            pltpu.VMEM((2, 2, 4, 4, 5, 8, LANES), BF),
+            pltpu.VMEM((2, 2, 2, 4, 2, 5, 8, LANES), BF),
             pltpu.VMEM((2, 3, 5, 8, LANES), BF),
-            pltpu.VMEM((2, 3, 40, 128), F32),
+            pltpu.VMEM((2, 8, 40, LANES), BF),
+            pltpu.VMEM((2, 7, 40, LANES), BF),
+            pltpu.VMEM((3, 320, 128), F32),
             pltpu.VMEM((2, 8, 8, LANES), BF),
             pltpu.VMEM((2, 7, 8, LANES), BF),
             pltpu.VMEM((OWN, CH), BF),
@@ -433,8 +562,8 @@
             dma((2, 5)),
             dma((2, 2, 4)),
             dma((2, 2, 4)),
-            dma((2, 3)),
-            dma((2, 3)),
+            dma((2, 7)),
+            dma((2, 7)),
             dma((2, 7)),
             dma((2, 7)),
             dma((2,)),
@@ -446,11 +575,24 @@
     )(
         latent.reshape(OWN, CH), taps(first_weight), taps(second_weight), cotangent.reshape(OWN, CH)
     )
+    out, latent_grad, first, second = pl.pallas_call(
+        finish_kernel,
+        out_shape=(
+            jax.ShapeDtypeStruct((OWN, CH), BF),
+            jax.ShapeDtypeStruct((OWN, CH), BF),
+            jax.ShapeDtypeStruct((5 * UNIT,), F32),
+            jax.ShapeDtypeStruct((5 * UNIT,), F32),
+        ),
+        in_specs=[any_spec, any_spec, vmem_spec, vmem_spec],
+        out_specs=(any_spec, any_spec, vmem_spec, vmem_spec),
+        scratch_shapes=[pltpu.VMEM((2, OWN, CH), BF), dma((2, 2)), dma((2, 2))],
+        name="finish",
+    )(out, latent_grad, first, second)
     return (
         out.reshape(1, ROWS, COLS, CH),
         latent_grad.reshape(1, ROWS, COLS, CH),
-        first[:5, :UNIT].reshape(-1),
-        second[:5, :UNIT].reshape(-1),
+        first,
+        second,
     )
 
 

time: 75.6 us -> 66.2 us (0.88)
  the two profiles are of different devices: /device:TPU:2 before, /device:TPU:8 now
where the time goes in v2:
time: 66.2 us; the launch traced here: 66 us
  Pallas kernels  65.2 us (98%)
  between operations  0.8 us (1%)
    pallas_call x1, Pallas kernels, local(): pl.pallas_call(kernel, out_shape=(jax.ShapeDtypeStruct((OWN, CH), BF), ja...  61.9 us
    pallas_call x1, Pallas kernels, local(): pl.pallas_call(finish_kernel, out_shape=(jax.ShapeDtypeStruct((OWN, CH),...  3.29 us

profile of v2, /device:TPU:8, one launch (start us, length us, event | category | flops | bytes accessed | tf_op | source)
XLA Modules:
  0.0 66.0 jit_solution(11743694027542660653)
XLA Ops:
  0.6 61.9 %conv_pair.1 = (bf16[512,320]{1,0:T(8,128)(2,1)}, bf16[512,320]{1,0:T(8,128)(2,1)}, f32[8,384]{1,0:T(8,128)}, f32[8,384]{1,0:T(8,128)}) custom-call(bf16[512,320]{1,0:T(8,128)(2,1)} %bitcast.12, bf16[3,960,320]{2,1,0:T(8,128)(2,1)} %bitcast.10, bf16[3,960,320]{2,1,0:T(8,128)(2,1)} %bitcast.11, bf16[512,320]{1,0:T(8,128)(2,1)} %bitcast.13), custom_call_target="tpu_custom_call" | custom-call | tf_op jit(solution)/shard_map/conv_pair/pallas_call | solution.py:518
  62.5 3.3 %finish.1 = (bf16[512,320]{1,0:T(8,128)(2,1)}, bf16[512,320]{1,0:T(8,128)(2,1)}, f32[1800]{0:T(1024)}, f32[1800]{0:T(1024)}) custom-call(bf16[512,320]{1,0:T(8,128)(2,1)} %get-tuple-element.12.out_hbm, bf16[512,320]{1,0:T(8,128)(2,1)} %get-tuple-element.13.lg_hbm, f32[8,384]{1,0:T(8,128)} %get-tuple-element.14.g1_ref, f32[8,384]{1,0:T(8,128)} %get-tuple-element.15.g2_ref), custom_call_target="tpu_custom_call" | custom-call | tf_op jit(solution)/shard_map/finish/pallas_call | solution.py:578

commit v3 on v2

--- a/solution.py
+++ b/solution.py
@@ -50,8 +50,8 @@
 def kernel(
     lat_hbm, w1_hbm, w2_hbm, cot_hbm, out_hbm, lg_hbm, g1_ref, g2_ref,
     latx, cotx, act, a3, c3, w1, w2, w1t, w2t, acc, slope, h3, hg3, terms, perm, lhs_t,
-    grid, core_recv, sums, zrecv, xrecv, late, mids, midr, sc, ys, yr, outv, lgv,
-    load_sem, halo_send, halo_recv, core_send, core_rsem, zsend, zrsem, lsend, lrsem, ysend, yrsem, store_sem,
+    grid, core_recv, sums, xrecv, late, mids, midr, sc, ys, yr, outv, lgv,
+    load_sem, halo_send, halo_recv, core_send, core_rsem, xsend, xrsem, lsend, lrsem, ysend, yrsem, store_sem,
 ):
     dp, space = lax.axis_index("dp"), lax.axis_index("space")
     yy, core = dp // 2, dp % 2
@@ -124,12 +124,18 @@
 
     loads[2].wait()
 
-    def conv_one(first, count):
-        size = count * COLS
-        total = dot(a3[first * COLS : first * COLS + size, :], w1[0])
-        total += dot(a3[(first + 1) * COLS : (first + 1) * COLS + size, :], w1[1])
-        total += dot(a3[(first + 2) * COLS : (first + 2) * COLS + size, :], w1[2])
-        acc[first * COLS : first * COLS + size, :] = total
+    def conv_one(runs):
+        def rows(i):
+            parts = [a3[(first + i) * COLS : (first + count + i) * COLS, :] for first, count in runs]
+            return parts[0] if len(parts) == 1 else jnp.concatenate(parts, axis=0)
+
+        total = dot(rows(0), w1[0])
+        total += dot(rows(1), w1[1])
+        total += dot(rows(2), w1[2])
+        at = 0
+        for first, count in runs:
+            acc[first * COLS : (first + count) * COLS, :] = total[at : at + count * COLS]
+            at += count * COLS
 
         def finish(k, _):
             at = pl.ds(pl.multiple_of(k * COLS, COLS), COLS)
@@ -139,9 +145,10 @@
             h3[at, :] = jnp.concatenate(column_shifts(hidden * sig), axis=1)
             return 0
 
-        lax.fori_loop(first, first + count, finish, 0)
-
-    conv_one(2, 6)
+        for first, count in runs:
+            lax.fori_loop(first, first + count, finish, 0)
+
+    conv_one([(2, 6)])
 
     @pl.when(space == 0)
     def _():
@@ -166,8 +173,7 @@
     for first in (0, 10):
         widen(latx, a3, first, first + 2, False, True)
         widen(cotx, c3, first, first + 2, True, False)
-    conv_one(0, 2)
-    conv_one(8, 2)
+    conv_one([(0, 2), (8, 2)])
 
     def clear_outside(ref):
         @pl.when(space == 0)
@@ -213,54 +219,35 @@
             part = grid[n, :, 4 * core + k].astype(F32) + core_recv[n, :, k].astype(F32)
             sums[n, k] = part.reshape(2, 4, 5, 8, LANES).astype(BF)
 
-    steps = (1, 7)
-
-    def zblock(ref, n, target, way, half):
-        lo, size = (2 * way, 2) if half else (0, 4)
-        return ref.at[n, target // 2, target % 2, pl.ds(lo, size)]
-
-    def zcopy(n, s, way):
-        target = (zz + steps[way] * (5 - s)) % 8
-        lo, size = (2 * way, 2) if s == 1 else (0, 4)
+    def xcopy(n, part, way):
+        step = 1 if way == 0 else 3
+        target = (xx + (2 * step if part == 1 else step)) % 4
+        lo = 2 * way if part < 3 else 2 - 2 * way
         return pltpu.make_async_remote_copy(
-            src_ref=zblock(sums, n, target, way, s == 1),
-            dst_ref=zrecv.at[n, way, s - 1, pl.ds(lo, size)],
-            send_sem=zsend.at[n, way, s - 1], recv_sem=zrsem.at[n, way, s - 1],
-            device_id=(dp, (zz + steps[way]) % 8 * 4 + xx), device_id_type=MESH)
-
-    def zstep(n, s):
+            src_ref=sums.at[n, pl.ds(lo, 2), :, target],
+            dst_ref=xrecv.at[n, way, min(part, 2) - 1, pl.ds(lo, 2)],
+            send_sem=xsend.at[n, way, part - 1], recv_sem=xrsem.at[n, way, part - 1],
+            device_id=(dp, zz * 4 + (xx + step) % 4), device_id_type=MESH)
+
+    def xstart(n):
+        for part in (1, 3):
+            for way in range(2):
+                xcopy(n, part, way).start()
+
+    def xstep(n):
         for way in range(2):
-            if s >= 2:
-                zcopy(n, s - 1, way).wait_recv()
-                ref = zblock(sums, n, (zz + steps[way] * (5 - s)) % 8, way, s == 2)
-                lo, size = (2 * way, 2) if s == 2 else (0, 4)
-                ref[...] = (ref[...].astype(F32) + zrecv[n, way, s - 2, lo : lo + size].astype(F32)).astype(BF)
-            zcopy(n, s, way).start()
-
-    def xcopy(n, s, way):
-        target = (xx + (1 if way == 0 else 3) * (3 - s)) % 4
-        lo, size = (2 * way, 2) if s == 1 else (0, 4)
+            xcopy(n, 1, way).wait_recv()
+            lo = 2 * way
+            ref = sums.at[n, pl.ds(lo, 2), :, (xx + (1 if way == 0 else 3)) % 4]
+            ref[...] = (ref[...].astype(F32) + xrecv[n, way, 0, lo : lo + 2].astype(F32)).astype(BF)
+            xcopy(n, 2, way).start()
+
+    def z_direct(n, d):
+        to = (zz + d) % 8
         return pltpu.make_async_remote_copy(
-            src_ref=sums.at[n, pl.ds(lo, size), :, target],
-            dst_ref=xrecv.at[n, way, s - 1, pl.ds(lo, size)],
-            send_sem=zsend.at[n, way, s - 1], recv_sem=zrsem.at[n, way, s - 1],
-            device_id=(dp, zz * 4 + (xx + (1 if way == 0 else 3)) % 4), device_id_type=MESH)
-
-    def xstep(n, s):
-        for way in range(2):
-            if s == 2:
-                xcopy(n, 1, way).wait_recv()
-                lo = 2 * way
-                ref = sums.at[n, pl.ds(lo, 2), :, (xx + (1 if way == 0 else 3)) % 4]
-                ref[...] = (ref[...].astype(F32) + xrecv[n, way, 0, lo : lo + 2].astype(F32)).astype(BF)
-            xcopy(n, s, way).start()
-
-    def x_direct(n, d):
-        to = (xx + d) % 4
-        return pltpu.make_async_remote_copy(
-            src_ref=sums.at[n, zz // 2, zz % 2, to], dst_ref=late.at[n, d - 1],
+            src_ref=sums.at[n, to // 2, to % 2, xx], dst_ref=late.at[n, d - 1],
             send_sem=lsend.at[n, d - 1], recv_sem=lrsem.at[n, d - 1],
-            device_id=(dp, zz * 4 + to), device_id_type=MESH)
+            device_id=(dp, to * 4 + xx), device_id_type=MESH)
 
     def y_direct(n, d):
         to = (yy + d) % 8
@@ -269,26 +256,29 @@
             send_sem=lsend.at[n, d - 1], recv_sem=lrsem.at[n, d - 1],
             device_id=(to * 2 + core, space), device_id_type=MESH)
 
-    def zfinal(n):
-        for way in range(2):
-            zcopy(n, 4, way).wait_recv()
-        ref = sums.at[n, zz // 2, zz % 2]
-        ref[...] = (ref[...].astype(F32) + zrecv[n, 0, 3].astype(F32) + zrecv[n, 1, 3].astype(F32)).astype(BF)
-        for d in range(1, 4):
-            x_direct(n, d).start()
-
     def xfinal(n):
         for way in range(2):
-            xcopy(n, 2, way).wait_recv()
-        total = sums[n, :, :, xx].astype(F32) + xrecv[n, 0, 1].astype(F32) + xrecv[n, 1, 1].astype(F32)
-        flat = total.reshape(40 * 8, LANES)
-        for k in range(3):
-            sc[k] = flat[:, 128 * k : 128 * k + 128]
-        for to in range(8):
+            for part in (2, 3):
+                xcopy(n, part, way).wait_recv()
+
+        @pl.when(core == 0)
+        def _():
+            ref = sums.at[n, :, :, xx]
+            ref[...] = (ref[...].astype(F32) + xrecv[n, 0, 1].astype(F32) + xrecv[n, 1, 1].astype(F32)).astype(BF)
+            for d in range(1, 8):
+                z_direct(n, d).start()
+
+        @pl.when(core == 1)
+        def _():
+            total = sums[n, :, :, xx].astype(F32) + xrecv[n, 0, 1].astype(F32) + xrecv[n, 1, 1].astype(F32)
+            flat = total.reshape(40 * 8, LANES)
             for k in range(3):
-                mids[n, to, :, 128 * k : 128 * k + 128] = sc[k, pl.ds(to, 40, stride=8), :].astype(BF)
-        for d in range(1, 8):
-            y_direct(n, d).start()
+                sc[k] = flat[:, 128 * k : 128 * k + 128]
+            for to in range(8):
+                for k in range(3):
+                    mids[n, to, :, 128 * k : 128 * k + 128] = sc[k, pl.ds(to, 40, stride=8), :].astype(BF)
+            for d in range(1, 8):
+                y_direct(n, d).start()
 
     def last_copy(n, d, over_y):
         if over_y:
@@ -302,10 +292,10 @@
             send_sem=ysend.at[n, d - 1], recv_sem=yrsem.at[n, d - 1],
             device_id=device, device_id_type=MESH)
 
-    def x_finish(n):
+    def z_finish(n):
         total = sums[n, zz // 2, zz % 2, xx].astype(F32)
-        for d in range(1, 4):
-            x_direct(n, d).wait_recv()
+        for d in range(1, 8):
+            z_direct(n, d).wait_recv()
             total += late[n, d - 1].astype(F32)
         flat = total.reshape(5 * 8, LANES)
         for k in range(3):
@@ -345,25 +335,14 @@
         def _():
             total_over(False)
 
-    def advance(n, step):
+    def middle(n):
         @pl.when(core == 0)
         def _():
-            if step <= 4:
-                zstep(n, step)
-            elif step == 5:
-                zfinal(n)
-            else:
-                x_finish(n)
-
-        if step in (1, 2, 3, 5):
-            @pl.when(core == 1)
-            def _():
-                if step <= 2:
-                    xstep(n, step)
-                elif step == 3:
-                    xfinal(n)
-                else:
-                    y_finish(n)
+            z_finish(n)
+
+        @pl.when(core == 1)
+        def _():
+            y_finish(n)
 
     ys[...] = jnp.zeros(ys.shape, BF)
     for i in range(3):
@@ -389,20 +368,19 @@
     clear_outside(hg3)
 
     core_sum(1)
-    advance(1, 1)
+    xstart(1)
 
     for i in range(3):
         left = dot_nt(perm[...], act[(i + 1) * COLS : (i + 1) * COLS + OWN, :]).astype(BF)
         terms[i, :, : 3 * CH] = dot(left, hg3[COLS : COLS + OWN, :])
     pack_terms(0)
-    advance(1, 2)
+    xstep(1)
 
     for i in range(3):
         w2t[i] = jnp.concatenate([w2[i, CH * j : CH * j + CH, :] for j in range(3)], axis=1)
         w1t[i] = jnp.concatenate([w1[i, CH * j : CH * j + CH, :] for j in range(3)], axis=1)
     core_sum(0)
-    advance(0, 1)
-    advance(1, 3)
+    xstart(0)
 
     total = dot_nt(h3[0:OWN, :], w2t[0])
     total += dot_nt(h3[COLS : COLS + OWN, :], w2t[1])
@@ -410,15 +388,13 @@
     outv[...] = total.astype(BF)
     store_out = pltpu.make_async_copy(outv, out_hbm, store_sem.at[0])
     store_out.start()
-    advance(0, 2)
-    advance(1, 4)
+    xfinal(1)
+    xstep(0)
 
     total = dot_nt(hg3[2 * COLS : 2 * COLS + OWN, :], w1t[0])
     total += dot_nt(hg3[COLS : COLS + OWN, :], w1t[1])
     total += dot_nt(hg3[0:OWN, :], w1t[2])
     acc[0:OWN, :] = total
-    advance(0, 3)
-    advance(1, 5)
 
     def finish_latent(k, _):
         at = pl.ds(pl.multiple_of(k * COLS, COLS), COLS)
@@ -430,12 +406,8 @@
     lax.fori_loop(0, 8, finish_latent, 0)
     store_lg = pltpu.make_async_copy(lgv, lg_hbm, store_sem.at[1])
     store_lg.start()
-    advance(0, 4)
-    advance(1, 6)
-    advance(0, 5)
-    advance(0, 6)
-    last(1, g2_ref)
-    last(0, g1_ref)
+    middle(1)
+    xfinal(0)
 
     @pl.when(space > 0)
     def _():
@@ -450,30 +422,36 @@
     for n in range(2):
         for r in range(5):
             core_copy(n, r).wait_send()
-
-    @pl.when(core == 0)
-    def _():
-        for n in range(2):
-            for way in range(2):
-                for s in range(1, 5):
-                    zcopy(n, s, way).wait_send()
-            for d in range(1, 4):
-                x_direct(n, d).wait_send()
-            for d in range(1, 8):
-                last_copy(n, d, True).wait_send()
-
-    @pl.when(core == 1)
-    def _():
-        for n in range(2):
-            for way in range(2):
-                for s in range(1, 3):
-                    xcopy(n, s, way).wait_send()
-            for d in range(1, 8):
-                y_direct(n, d).wait_send()
-                last_copy(n, d, False).wait_send()
-
+        for way in range(2):
+            for part in (1, 2, 3):
+                xcopy(n, part, way).wait_send()
     store_out.wait()
     store_lg.wait()
+    middle(0)
+
+    def sent(copy):
+        for n in range(2):
+            for d in range(1, 8):
+                copy(n, d).wait_send()
+
+    @pl.when(core == 0)
+    def _():
+        sent(z_direct)
+
+    @pl.when(core == 1)
+    def _():
+        sent(y_direct)
+
+    last(1, g2_ref)
+    last(0, g1_ref)
+
+    @pl.when(core == 0)
+    def _():
+        sent(lambda n, d: last_copy(n, d, True))
+
+    @pl.when(core == 1)
+    def _():
+        sent(lambda n, d: last_copy(n, d, False))
 
 
 def finish_kernel(out_hbm, lg_hbm, g1_ref, g2_ref, out_res, lg_res, f1_ref, f2_ref, buf, sem_in, sem_out):
@@ -545,9 +523,8 @@
             pltpu.VMEM((2, UNITS, 8, 8, LANES), BF),
             pltpu.VMEM((2, UNITS, 4, 8, LANES), BF),
             pltpu.VMEM((2, 4, 2, 4, 5, 8, LANES), BF),
-            pltpu.VMEM((2, 2, 4, 4, 5, 8, LANES), BF),
             pltpu.VMEM((2, 2, 2, 4, 2, 5, 8, LANES), BF),
-            pltpu.VMEM((2, 3, 5, 8, LANES), BF),
+            pltpu.VMEM((2, 7, 5, 8, LANES), BF),
             pltpu.VMEM((2, 8, 40, LANES), BF),
             pltpu.VMEM((2, 7, 40, LANES), BF),
             pltpu.VMEM((3, 320, 128), F32),
@@ -560,8 +537,8 @@
             dma((4,)),
             dma((2, 5)),
             dma((2, 5)),
-            dma((2, 2, 4)),
-            dma((2, 2, 4)),
+            dma((2, 2, 3)),
+            dma((2, 2, 3)),
             dma((2, 7)),
             dma((2, 7)),
             dma((2, 7)),

time: 66.2 us -> 65.1 us (0.983)
  the two profiles are of different devices: /device:TPU:8 before, /device:TPU:4 now
where the time goes in v3:
time: 65.1 us; the launch traced here: 64.9 us
  Pallas kernels  64.1 us (98%)
  between operations  0.8 us (1%)
    pallas_call x1, Pallas kernels, local(): pl.pallas_call(kernel, out_shape=(jax.ShapeDtypeStruct((OWN, CH), BF), ja...  60.8 us
    pallas_call x1, Pallas kernels, local(): pl.pallas_call(finish_kernel, out_shape=(jax.ShapeDtypeStruct((OWN, CH),...  3.29 us

profile of v3, /device:TPU:4, one launch (start us, length us, event | category | flops | bytes accessed | tf_op | source)
XLA Modules:
  0.0 64.9 jit_solution(15720676601906450259)
XLA Ops:
  0.6 60.8 %conv_pair.1 = (bf16[512,320]{1,0:T(8,128)(2,1)}, bf16[512,320]{1,0:T(8,128)(2,1)}, f32[8,384]{1,0:T(8,128)}, f32[8,384]{1,0:T(8,128)}) custom-call(bf16[512,320]{1,0:T(8,128)(2,1)} %bitcast.12, bf16[3,960,320]{2,1,0:T(8,128)(2,1)} %bitcast.10, bf16[3,960,320]{2,1,0:T(8,128)(2,1)} %bitcast.11, bf16[512,320]{1,0:T(8,128)(2,1)} %bitcast.13), custom_call_target="tpu_custom_call" | custom-call | tf_op jit(solution)/shard_map/conv_pair/pallas_call | solution.py:496
  61.4 3.3 %finish.1 = (bf16[512,320]{1,0:T(8,128)(2,1)}, bf16[512,320]{1,0:T(8,128)(2,1)}, f32[1800]{0:T(1024)}, f32[1800]{0:T(1024)}) custom-call(bf16[512,320]{1,0:T(8,128)(2,1)} %get-tuple-element.12.out_hbm, bf16[512,320]{1,0:T(8,128)(2,1)} %get-tuple-element.13.lg_hbm, f32[8,384]{1,0:T(8,128)} %get-tuple-element.14.g1_ref, f32[8,384]{1,0:T(8,128)} %get-tuple-element.15.g2_ref), custom_call_target="tpu_custom_call" | custom-call | tf_op jit(solution)/shard_map/finish/pallas_call | solution.py:555

commit v4 on v3

--- a/solution.py
+++ b/solution.py
@@ -49,7 +49,7 @@
 
 def kernel(
     lat_hbm, w1_hbm, w2_hbm, cot_hbm, out_hbm, lg_hbm, g1_ref, g2_ref,
-    latx, cotx, act, a3, c3, w1, w2, w1t, w2t, acc, slope, h3, hg3, terms, perm, lhs_t,
+    latx, cotx, act, a3, c3, w1, w2, w1t, w2t, acc, slope, h3, hg3, terms, perm, lhs_t, mid_t,
     grid, core_recv, sums, xrecv, late, mids, midr, sc, ys, yr, outv, lgv,
     load_sem, halo_send, halo_recv, core_send, core_rsem, xsend, xrsem, lsend, lrsem, ysend, yrsem, store_sem,
 ):
@@ -121,6 +121,7 @@
     group = ((row % 8) * 2 + row // 32 % 2) * 4 + row // 8 % 4
     perm[...] = jnp.where(chan == 5 * group + row // 64, 1.0, 0.0).astype(BF)
     lhs_t[...] = dot_nt(perm[...], cotx[2 * COLS : 10 * COLS, :]).astype(BF)
+    mid_t[...] = dot_nt(perm[...], act[2 * COLS : 10 * COLS, :]).astype(BF)
 
     loads[2].wait()
 
@@ -353,28 +354,42 @@
     pack_terms(1)
 
     loads[3].wait()
-    total = dot(c3[2 * COLS : 2 * COLS + MID, :], w2[0])
-    total += dot(c3[COLS : COLS + MID, :], w2[1])
-    total += dot(c3[0:MID, :], w2[2])
-    acc[...] = total
-
-    def finish_back(k, _):
-        at = pl.ds(pl.multiple_of(k * COLS, COLS), COLS)
-        before, here, after = column_shifts(acc[at, :] * slope[at, :])
-        hg3[at, :] = jnp.concatenate([after, here, before], axis=1)
-        return 0
-
-    lax.fori_loop(0, 10, finish_back, 0)
-    clear_outside(hg3)
+    def conv_back(runs):
+        def rows(i):
+            parts = [c3[(first + i) * COLS : (first + count + i) * COLS, :] for first, count in runs]
+            return parts[0] if len(parts) == 1 else jnp.concatenate(parts, axis=0)
+
+        total = dot(rows(2), w2[0])
+        total += dot(rows(1), w2[1])
+        total += dot(rows(0), w2[2])
+        at = 0
+        for first, count in runs:
+            acc[first * COLS : (first + count) * COLS, :] = total[at : at + count * COLS]
+            at += count * COLS
+
+        def finish(k, _):
+            at = pl.ds(pl.multiple_of(k * COLS, COLS), COLS)
+            before, here, after = column_shifts(acc[at, :] * slope[at, :])
+            hg3[at, :] = jnp.concatenate([after, here, before], axis=1)
+            return 0
+
+        for first, count in runs:
+            lax.fori_loop(first, first + count, finish, 0)
+
+    conv_back([(1, 8)])
 
     core_sum(1)
     xstart(1)
 
     for i in range(3):
-        left = dot_nt(perm[...], act[(i + 1) * COLS : (i + 1) * COLS + OWN, :]).astype(BF)
-        terms[i, :, : 3 * CH] = dot(left, hg3[COLS : COLS + OWN, :])
+        if i != 1:
+            lhs_t[...] = dot_nt(perm[...], act[(i + 1) * COLS : (i + 1) * COLS + OWN, :]).astype(BF)
+        left = mid_t if i == 1 else lhs_t
+        terms[i, :, : 3 * CH] = dot(left[...], hg3[COLS : COLS + OWN, :])
     pack_terms(0)
     xstep(1)
+    conv_back([(0, 1), (9, 1)])
+    clear_outside(hg3)
 
     for i in range(3):
         w2t[i] = jnp.concatenate([w2[i, CH * j : CH * j + CH, :] for j in range(3)], axis=1)
@@ -454,7 +469,17 @@
         sent(lambda n, d: last_copy(n, d, False))
 
 
-def finish_kernel(out_hbm, lg_hbm, g1_ref, g2_ref, out_res, lg_res, f1_ref, f2_ref, buf, sem_in, sem_out):
+def finish_kernel(out_hbm, lg_hbm, g1_hbm, g2_hbm, out_res, lg_res, f1_res, f2_res, buf, share, f1, f2, sem_in, sem_out):
+    shares = [
+        pltpu.make_async_copy(g1_hbm, share.at[0], sem_in.at[2, 0]),
+        pltpu.make_async_copy(g2_hbm, share.at[1], sem_in.at[2, 1]),
+    ]
+    flats = [
+        pltpu.make_async_copy(f1, f1_res, sem_out.at[2, 0]),
+        pltpu.make_async_copy(f2, f2_res, sem_out.at[2, 1]),
+    ]
+    for copy in shares:
+        copy.start()
     takes, puts = [], []
     for n, (src, dst) in enumerate(((out_hbm, out_res), (lg_hbm, lg_res))):
         for k in range(2):
@@ -463,11 +488,11 @@
             puts.append(pltpu.make_async_copy(buf.at[n, at], dst.at[at], sem_out.at[n, k]))
     for take in takes:
         take.start()
-    for take, put in zip(takes, puts):
-        take.wait()
-        put.start()
+    for copy in shares:
+        copy.wait()
     lane = lax.broadcasted_iota(jnp.int32, (1, 128), 1)
-    for src, dst in ((g1_ref, f1_ref), (g2_ref, f2_ref)):
+    for n, dst in enumerate((f1, f2)):
+        src = share.at[n]
         for k in range(15):
             start, end = 128 * k, min(128 * k + 128, 5 * UNIT)
             size, value, at = end - start, None, start
@@ -482,8 +507,12 @@
                 value = piece if value is None else jnp.where(lane < at - start, value, piece)
                 at += min(UNIT - col, end - at)
             dst[pl.ds(start, size)] = value[0, :size]
-    for put in puts:
-        put.wait()
+        flats[n].start()
+    for take, put in zip(takes, puts):
+        take.wait()
+        put.start()
+    for copy in puts + flats:
+        copy.wait()
 
 
 def local(latent, first_weight, second_weight, cotangent):
@@ -519,6 +548,7 @@
             pltpu.VMEM((MID, 3 * CH), BF),
             pltpu.VMEM((3, CH, 1024), F32),
             pltpu.VMEM((CH, CH), BF),
+            pltpu.VMEM((CH, OWN), BF),
             pltpu.VMEM((CH, OWN), BF),
             pltpu.VMEM((2, UNITS, 8, 8, LANES), BF),
             pltpu.VMEM((2, UNITS, 4, 8, LANES), BF),
@@ -560,9 +590,16 @@
             jax.ShapeDtypeStruct((5 * UNIT,), F32),
             jax.ShapeDtypeStruct((5 * UNIT,), F32),
         ),
-        in_specs=[any_spec, any_spec, vmem_spec, vmem_spec],
-        out_specs=(any_spec, any_spec, vmem_spec, vmem_spec),
-        scratch_shapes=[pltpu.VMEM((2, OWN, CH), BF), dma((2, 2)), dma((2, 2))],
+        in_specs=[any_spec] * 4,
+        out_specs=(any_spec,) * 4,
+        scratch_shapes=[
+            pltpu.VMEM((2, OWN, CH), BF),
+            pltpu.VMEM((2, 8, LANES), F32),
+            pltpu.VMEM((5 * UNIT,), F32),
+            pltpu.VMEM((5 * UNIT,), F32),
+            dma((3, 2)),
+            dma((3, 2)),
+        ],
         name="finish",
     )(out, latent_grad, first, second)
     return (

time: 65.1 us -> 64 us (0.983)
  Pallas kernels: 64.1 us -> 63 us
    pallas_call x1, Pallas kernels: 3.29 us -> 2.03 us  [local(): pl.pallas_call(finish_kernel, out_shape=(jax.ShapeDtypeStruct((OWN, CH),...]
where the time goes in v4:
time: 64 us; the launch traced here: 63.8 us
  Pallas kernels  63 us (98%)
  between operations  0.8 us (1%)
    pallas_call x1, Pallas kernels, local(): pl.pallas_call(kernel, out_shape=(jax.ShapeDtypeStruct((OWN, CH), BF), ja...  60.9 us
    pallas_call x1, Pallas kernels, local(): pl.pallas_call(finish_kernel, out_shape=(jax.ShapeDtypeStruct((OWN, CH),...  2.03 us

profile of v4, /device:TPU:4, one launch (start us, length us, event | category | flops | bytes accessed | tf_op | source)
XLA Modules:
  0.0 63.8 jit_solution(14962930177526857597)
XLA Ops:
  0.6 60.9 %conv_pair.1 = (bf16[512,320]{1,0:T(8,128)(2,1)}, bf16[512,320]{1,0:T(8,128)(2,1)}, f32[8,384]{1,0:T(8,128)}, f32[8,384]{1,0:T(8,128)}) custom-call(bf16[512,320]{1,0:T(8,128)(2,1)} %bitcast.12, bf16[3,960,320]{2,1,0:T(8,128)(2,1)} %bitcast.10, bf16[3,960,320]{2,1,0:T(8,128)(2,1)} %bitcast.11, bf16[512,320]{1,0:T(8,128)(2,1)} %bitcast.13), custom_call_target="tpu_custom_call" | custom-call | tf_op jit(solution)/shard_map/conv_pair/pallas_call | solution.py:525
  61.6 2.0 %finish.1 = (bf16[512,320]{1,0:T(8,128)(2,1)}, bf16[512,320]{1,0:T(8,128)(2,1)}, f32[1800]{0:T(1024)}, f32[1800]{0:T(1024)}) custom-call(bf16[512,320]{1,0:T(8,128)(2,1)} %get-tuple-element.12.out_hbm, bf16[512,320]{1,0:T(8,128)(2,1)} %get-tuple-element.13.lg_hbm, f32[8,384]{1,0:T(8,128)} %get-tuple-element.14.g1_hbm, f32[8,384]{1,0:T(8,128)} %get-tuple-element.15.g2_hbm), custom_call_target="tpu_custom_call" | custom-call | tf_op jit(solution)/shard_map/finish/pallas_call | solution.py:585

commit v5 on v4

--- a/solution.py
+++ b/solution.py
@@ -18,6 +18,7 @@
 UNIT = 360
 LANES = 384
 UNITS = 40
+FAR_FIRST = (4, 3, 5, 2, 6, 1, 7)
 
 
 def dot(a, b):
@@ -266,7 +267,7 @@
         def _():
             ref = sums.at[n, :, :, xx]
             ref[...] = (ref[...].astype(F32) + xrecv[n, 0, 1].astype(F32) + xrecv[n, 1, 1].astype(F32)).astype(BF)
-            for d in range(1, 8):
+            for d in FAR_FIRST:
                 z_direct(n, d).start()
 
         @pl.when(core == 1)
@@ -278,7 +279,7 @@
             for to in range(8):
                 for k in range(3):
                     mids[n, to, :, 128 * k : 128 * k + 128] = sc[k, pl.ds(to, 40, stride=8), :].astype(BF)
-            for d in range(1, 8):
+            for d in FAR_FIRST:
                 y_direct(n, d).start()
 
     def last_copy(n, d, over_y):
@@ -304,7 +305,7 @@
         for to in range(8):
             for k in range(3):
                 ys[n, to, 0:5, 128 * k : 128 * k + 128] = sc[k, pl.ds(to, 5, stride=8), :].astype(BF)
-        for d in range(1, 8):
+        for d in FAR_FIRST:
             last_copy(n, d, True).start()
 
     def y_finish(n):
@@ -317,7 +318,7 @@
         for to in range(8):
             for k in range(3):
                 ys[n, to, 0:5, 128 * k : 128 * k + 128] = sc[k, 5 * to : 5 * to + 5, :].astype(BF)
-        for d in range(1, 8):
+        for d in FAR_FIRST:
             last_copy(n, d, False).start()
 
     def last(n, ref):
@@ -388,8 +389,6 @@
         terms[i, :, : 3 * CH] = dot(left[...], hg3[COLS : COLS + OWN, :])
     pack_terms(0)
     xstep(1)
-    conv_back([(0, 1), (9, 1)])
-    clear_outside(hg3)
 
     for i in range(3):
         w2t[i] = jnp.concatenate([w2[i, CH * j : CH * j + CH, :] for j in range(3)], axis=1)
@@ -405,6 +404,8 @@
     store_out.start()
     xfinal(1)
     xstep(0)
+    conv_back([(0, 1), (9, 1)])
+    clear_outside(hg3)
 
     total = dot_nt(hg3[2 * COLS : 2 * COLS + OWN, :], w1t[0])
     total += dot_nt(hg3[COLS : COLS + OWN, :], w1t[1])

time: 64 us -> 61.9 us (0.967)
  the two profiles are of different devices: /device:TPU:4 before, /device:TPU:8 now
where the time goes in v5:
time: 61.9 us; the launch traced here: 61.6 us
  Pallas kernels  60.8 us (98%)
  between operations  0.8 us (1%)
    pallas_call x1, Pallas kernels, local(): pl.pallas_call(kernel, out_shape=(jax.ShapeDtypeStruct((OWN, CH), BF), ja...  58.8 us
    pallas_call x1, Pallas kernels, local(): pl.pallas_call(finish_kernel, out_shape=(jax.ShapeDtypeStruct((OWN, CH),...  2.03 us

profile of v5, /device:TPU:8, one launch (start us, length us, event | category | flops | bytes accessed | tf_op | source)
XLA Modules:
  0.0 61.6 jit_solution(11461170790998787694)
XLA Ops:
  0.6 58.8 %conv_pair.1 = (bf16[512,320]{1,0:T(8,128)(2,1)}, bf16[512,320]{1,0:T(8,128)(2,1)}, f32[8,384]{1,0:T(8,128)}, f32[8,384]{1,0:T(8,128)}) custom-call(bf16[512,320]{1,0:T(8,128)(2,1)} %bitcast.12, bf16[3,960,320]{2,1,0:T(8,128)(2,1)} %bitcast.10, bf16[3,960,320]{2,1,0:T(8,128)(2,1)} %bitcast.11, bf16[512,320]{1,0:T(8,128)(2,1)} %bitcast.13), custom_call_target="tpu_custom_call" | custom-call | tf_op jit(solution)/shard_map/conv_pair/pallas_call | solution.py:526
  59.4 2.0 %finish.1 = (bf16[512,320]{1,0:T(8,128)(2,1)}, bf16[512,320]{1,0:T(8,128)(2,1)}, f32[1800]{0:T(1024)}, f32[1800]{0:T(1024)}) custom-call(bf16[512,320]{1,0:T(8,128)(2,1)} %get-tuple-element.12.out_hbm, bf16[512,320]{1,0:T(8,128)(2,1)} %get-tuple-element.13.lg_hbm, f32[8,384]{1,0:T(8,128)} %get-tuple-element.14.g1_hbm, f32[8,384]{1,0:T(8,128)} %get-tuple-element.15.g2_hbm), custom_call_target="tpu_custom_call" | custom-call | tf_op jit(solution)/shard_map/finish/pallas_call | solution.py:586

commit v6 on v5

--- a/solution.py
+++ b/solution.py
@@ -51,8 +51,8 @@
 def kernel(
     lat_hbm, w1_hbm, w2_hbm, cot_hbm, out_hbm, lg_hbm, g1_ref, g2_ref,
     latx, cotx, act, a3, c3, w1, w2, w1t, w2t, acc, slope, h3, hg3, terms, perm, lhs_t, mid_t,
-    grid, core_recv, sums, xrecv, late, mids, midr, sc, ys, yr, outv, lgv,
-    load_sem, halo_send, halo_recv, core_send, core_rsem, xsend, xrsem, lsend, lrsem, ysend, yrsem, store_sem,
+    grid, core_recv, sums, zrecv, xrecv, late, mids, midr, sc, ys, yr, outv, lgv,
+    load_sem, halo_send, halo_recv, core_send, core_rsem, zsend, zrsem, xsend, xrsem, lsend, lrsem, ysend, yrsem, store_sem,
 ):
     dp, space = lax.axis_index("dp"), lax.axis_index("space")
     yy, core = dp // 2, dp % 2
@@ -244,6 +244,44 @@
             ref[...] = (ref[...].astype(F32) + xrecv[n, way, 0, lo : lo + 2].astype(F32)).astype(BF)
             xcopy(n, 2, way).start()
 
+    steps = (1, 7)
+
+    def zblock(target, way, half):
+        lo, size = (2 * way, 2) if half else (0, 4)
+        return sums.at[1, target // 2, target % 2, pl.ds(lo, size)]
+
+    def zcopy(step, way):
+        target = (zz + steps[way] * (5 - step)) % 8
+        lo, size = (2 * way, 2) if step == 1 else (0, 4)
+        return pltpu.make_async_remote_copy(
+            src_ref=zblock(target, way, step == 1), dst_ref=zrecv.at[way, step - 1, pl.ds(lo, size)],
+            send_sem=zsend.at[way, step - 1], recv_sem=zrsem.at[way, step - 1],
+            device_id=(dp, (zz + steps[way]) % 8 * 4 + xx), device_id_type=MESH)
+
+    def zstep(step):
+        for way in range(2):
+            if step >= 2:
+                zcopy(step - 1, way).wait_recv()
+                ref = zblock((zz + steps[way] * (5 - step)) % 8, way, step == 2)
+                lo, size = (2 * way, 2) if step == 2 else (0, 4)
+                ref[...] = (ref[...].astype(F32) + zrecv[way, step - 2, lo : lo + size].astype(F32)).astype(BF)
+            zcopy(step, way).start()
+
+    def x_direct(d):
+        to = (xx + d) % 4
+        return pltpu.make_async_remote_copy(
+            src_ref=sums.at[1, zz // 2, zz % 2, to], dst_ref=late.at[1, d - 1],
+            send_sem=lsend.at[1, d - 1], recv_sem=lrsem.at[1, d - 1],
+            device_id=(dp, zz * 4 + to), device_id_type=MESH)
+
+    def zfinal():
+        for way in range(2):
+            zcopy(4, way).wait_recv()
+        ref = sums.at[1, zz // 2, zz % 2]
+        ref[...] = (ref[...].astype(F32) + zrecv[0, 3].astype(F32) + zrecv[1, 3].astype(F32)).astype(BF)
+        for d in (2, 1, 3):
+            x_direct(d).start()
+
     def z_direct(n, d):
         to = (zz + d) % 8
         return pltpu.make_async_remote_copy(
@@ -294,10 +332,10 @@
             send_sem=ysend.at[n, d - 1], recv_sem=yrsem.at[n, d - 1],
             device_id=device, device_id_type=MESH)
 
-    def z_finish(n):
+    def late_finish(n):
         total = sums[n, zz // 2, zz % 2, xx].astype(F32)
-        for d in range(1, 8):
-            z_direct(n, d).wait_recv()
+        for d in range(1, 4 if n else 8):
+            (x_direct(d) if n else z_direct(n, d)).wait_recv()
             total += late[n, d - 1].astype(F32)
         flat = total.reshape(5 * 8, LANES)
         for k in range(3):
@@ -337,10 +375,14 @@
         def _():
             total_over(False)
 
+    def by_core(zero, one):
+        pl.when(core == 0)(zero)
+        pl.when(core == 1)(one)
+
     def middle(n):
         @pl.when(core == 0)
         def _():
-            z_finish(n)
+            late_finish(n)
 
         @pl.when(core == 1)
         def _():
@@ -380,7 +422,7 @@
     conv_back([(1, 8)])
 
     core_sum(1)
-    xstart(1)
+    by_core(lambda: zstep(1), lambda: xstart(1))
 
     for i in range(3):
         if i != 1:
@@ -388,7 +430,7 @@
         left = mid_t if i == 1 else lhs_t
         terms[i, :, : 3 * CH] = dot(left[...], hg3[COLS : COLS + OWN, :])
     pack_terms(0)
-    xstep(1)
+    by_core(lambda: zstep(2), lambda: xstep(1))
 
     for i in range(3):
         w2t[i] = jnp.concatenate([w2[i, CH * j : CH * j + CH, :] for j in range(3)], axis=1)
@@ -402,9 +444,10 @@
     outv[...] = total.astype(BF)
     store_out = pltpu.make_async_copy(outv, out_hbm, store_sem.at[0])
     store_out.start()
-    xfinal(1)
+    by_core(lambda: zstep(3), lambda: xfinal(1))
     xstep(0)
     conv_back([(0, 1), (9, 1)])
+    pl.when(core == 0)(lambda: zstep(4))
     clear_outside(hg3)
 
     total = dot_nt(hg3[2 * COLS : 2 * COLS + OWN, :], w1t[0])
@@ -422,7 +465,7 @@
     lax.fori_loop(0, 8, finish_latent, 0)
     store_lg = pltpu.make_async_copy(lgv, lg_hbm, store_sem.at[1])
     store_lg.start()
-    middle(1)
+    by_core(zfinal, lambda: y_finish(1))
     xfinal(0)
 
     @pl.when(space > 0)
@@ -438,11 +481,22 @@
     for n in range(2):
         for r in range(5):
             core_copy(n, r).wait_send()
+
+    def sent_x(n):
         for way in range(2):
             for part in (1, 2, 3):
                 xcopy(n, part, way).wait_send()
+
+    def sent_z():
+        for way in range(2):
+            for step in range(1, 5):
+                zcopy(step, way).wait_send()
+
+    sent_x(0)
+    by_core(sent_z, lambda: sent_x(1))
     store_out.wait()
     store_lg.wait()
+    pl.when(core == 0)(lambda: late_finish(1))
     middle(0)
 
     def sent(copy):
@@ -452,7 +506,10 @@
 
     @pl.when(core == 0)
     def _():
-        sent(z_direct)
+        for d in range(1, 8):
+            z_direct(0, d).wait_send()
+        for d in range(1, 4):
+            x_direct(d).wait_send()
 
     @pl.when(core == 1)
     def _():
@@ -554,6 +611,7 @@
             pltpu.VMEM((2, UNITS, 8, 8, LANES), BF),
             pltpu.VMEM((2, UNITS, 4, 8, LANES), BF),
             pltpu.VMEM((2, 4, 2, 4, 5, 8, LANES), BF),
+            pltpu.VMEM((2, 4, 4, 5, 8, LANES), BF),
             pltpu.VMEM((2, 2, 2, 4, 2, 5, 8, LANES), BF),
             pltpu.VMEM((2, 7, 5, 8, LANES), BF),
             pltpu.VMEM((2, 8, 40, LANES), BF),
@@ -568,6 +626,8 @@
             dma((4,)),
             dma((2, 5)),
             dma((2, 5)),
+            dma((2, 4)),
+            dma((2, 4)),
             dma((2, 2, 3)),
             dma((2, 2, 3)),
             dma((2, 7)),

time: 61.9 us -> 59.6 us (0.963)
  Pallas kernels: 60.8 us -> 58.6 us
    pallas_call x1, Pallas kernels: 58.8 us -> 56.6 us  [local(): pl.pallas_call(kernel, out_shape=(jax.ShapeDtypeStruct((OWN, CH), BF), ja...]
where the time goes in v6:
time: 59.6 us; the launch traced here: 59.4 us
  Pallas kernels  58.6 us (98%)
  between operations  0.8 us (1%)
    pallas_call x1, Pallas kernels, local(): pl.pallas_call(kernel, out_shape=(jax.ShapeDtypeStruct((OWN, CH), BF), ja...  56.6 us
    pallas_call x1, Pallas kernels, local(): pl.pallas_call(finish_kernel, out_shape=(jax.ShapeDtypeStruct((OWN, CH),...  2.03 us

profile of v6, /device:TPU:8, one launch (start us, length us, event | category | flops | bytes accessed | tf_op | source)
XLA Modules:
  0.0 59.4 jit_solution(18101674869520868437)
XLA Ops:
  0.6 56.6 %conv_pair.1 = (bf16[512,320]{1,0:T(8,128)(2,1)}, bf16[512,320]{1,0:T(8,128)(2,1)}, f32[8,384]{1,0:T(8,128)}, f32[8,384]{1,0:T(8,128)}) custom-call(bf16[512,320]{1,0:T(8,128)(2,1)} %bitcast.12, bf16[3,960,320]{2,1,0:T(8,128)(2,1)} %bitcast.10, bf16[3,960,320]{2,1,0:T(8,128)(2,1)} %bitcast.11, bf16[512,320]{1,0:T(8,128)(2,1)} %bitcast.13), custom_call_target="tpu_custom_call" | custom-call | tf_op jit(solution)/shard_map/conv_pair/pallas_call | solution.py:583
  57.3 2.0 %finish.1 = (bf16[512,320]{1,0:T(8,128)(2,1)}, bf16[512,320]{1,0:T(8,128)(2,1)}, f32[1800]{0:T(1024)}, f32[1800]{0:T(1024)}) custom-call(bf16[512,320]{1,0:T(8,128)(2,1)} %get-tuple-element.12.out_hbm, bf16[512,320]{1,0:T(8,128)(2,1)} %get-tuple-element.13.lg_hbm, f32[8,384]{1,0:T(8,128)} %get-tuple-element.14.g1_hbm, f32[8,384]{1,0:T(8,128)} %get-tuple-element.15.g2_hbm), custom_call_target="tpu_custom_call" | custom-call | tf_op jit(solution)/shard_map/finish/pallas_call | solution.py:646

commit v7 on v6

--- a/solution.py
+++ b/solution.py
@@ -151,6 +151,9 @@
             lax.fori_loop(first, first + count, finish, 0)
 
     conv_one([(2, 6)])
+    ys[...] = jnp.zeros(ys.shape, BF)
+    for i in range(3):
+        terms[i, :, 3 * CH :] = jnp.zeros((CH, 64), F32)
 
     @pl.when(space == 0)
     def _():
@@ -388,10 +391,6 @@
         def _():
             y_finish(n)
 
-    ys[...] = jnp.zeros(ys.shape, BF)
-    for i in range(3):
-        terms[i, :, 3 * CH :] = jnp.zeros((CH, 64), F32)
-
     for i in range(3):
         terms[i, :, : 3 * CH] = dot(lhs_t[...], h3[i * COLS : i * COLS + OWN, :])
     pack_terms(1)
@@ -432,11 +431,12 @@
     pack_terms(0)
     by_core(lambda: zstep(2), lambda: xstep(1))
 
+    core_sum(0)
+    xstart(0)
+
     for i in range(3):
         w2t[i] = jnp.concatenate([w2[i, CH * j : CH * j + CH, :] for j in range(3)], axis=1)
         w1t[i] = jnp.concatenate([w1[i, CH * j : CH * j + CH, :] for j in range(3)], axis=1)
-    core_sum(0)
-    xstart(0)
 
     total = dot_nt(h3[0:OWN, :], w2t[0])
     total += dot_nt(h3[COLS : COLS + OWN, :], w2t[1])

time: 59.6 us -> 60.2 us (1.010)
  no operation moved by 1% of the time
where the time goes in v7:
time: 60.2 us; the launch traced here: 60 us
  Pallas kernels  59.2 us (98%)
  between operations  0.8 us (1%)
    pallas_call x1, Pallas kernels, local(): pl.pallas_call(kernel, out_shape=(jax.ShapeDtypeStruct((OWN, CH), BF), ja...  57.1 us
    pallas_call x1, Pallas kernels, local(): pl.pallas_call(finish_kernel, out_shape=(jax.ShapeDtypeStruct((OWN, CH),...  2.03 us

profile of v7, /device:TPU:8, one launch (start us, length us, event | category | flops | bytes accessed | tf_op | source)
XLA Modules:
  0.0 60.0 jit_solution(7855386861734016041)
XLA Ops:
  0.6 57.1 %conv_pair.1 = (bf16[512,320]{1,0:T(8,128)(2,1)}, bf16[512,320]{1,0:T(8,128)(2,1)}, f32[8,384]{1,0:T(8,128)}, f32[8,384]{1,0:T(8,128)}) custom-call(bf16[512,320]{1,0:T(8,128)(2,1)} %bitcast.12, bf16[3,960,320]{2,1,0:T(8,128)(2,1)} %bitcast.10, bf16[3,960,320]{2,1,0:T(8,128)(2,1)} %bitcast.11, bf16[512,320]{1,0:T(8,128)(2,1)} %bitcast.13), custom_call_target="tpu_custom_call" | custom-call | tf_op jit(solution)/shard_map/conv_pair/pallas_call | solution.py:583
  57.8 2.0 %finish.1 = (bf16[512,320]{1,0:T(8,128)(2,1)}, bf16[512,320]{1,0:T(8,128)(2,1)}, f32[1800]{0:T(1024)}, f32[1800]{0:T(1024)}) custom-call(bf16[512,320]{1,0:T(8,128)(2,1)} %get-tuple-element.12.out_hbm, bf16[512,320]{1,0:T(8,128)(2,1)} %get-tuple-element.13.lg_hbm, f32[8,384]{1,0:T(8,128)} %get-tuple-element.14.g1_hbm, f32[8,384]{1,0:T(8,128)} %get-tuple-element.15.g2_hbm), custom_call_target="tpu_custom_call" | custom-call | tf_op jit(solution)/shard_map/finish/pallas_call | solution.py:646

commit v8 on v6

--- a/solution.py
+++ b/solution.py
@@ -465,8 +465,8 @@
     lax.fori_loop(0, 8, finish_latent, 0)
     store_lg = pltpu.make_async_copy(lgv, lg_hbm, store_sem.at[1])
     store_lg.start()
+    xfinal(0)
     by_core(zfinal, lambda: y_finish(1))
-    xfinal(0)
 
     @pl.when(space > 0)
     def _():

time: 59.6 us -> 58.8 us (0.987)
  the two profiles are of different devices: /device:TPU:8 before, /device:TPU:1 now
where the time goes in v8:
time: 58.8 us; the launch traced here: 58.6 us
  Pallas kernels  57.8 us (98%)
  between operations  0.8 us (1%)
    pallas_call x1, Pallas kernels, local(): pl.pallas_call(kernel, out_shape=(jax.ShapeDtypeStruct((OWN, CH), BF), ja...  55.7 us
    pallas_call x1, Pallas kernels, local(): pl.pallas_call(finish_kernel, out_shape=(jax.ShapeDtypeStruct((OWN, CH),...  2.03 us

profile of v8, /device:TPU:1, one launch (start us, length us, event | category | flops | bytes accessed | tf_op | source)
XLA Modules:
  0.0 58.6 jit_solution(4284618520732151597)
XLA Ops:
  0.6 55.7 %conv_pair.1 = (bf16[512,320]{1,0:T(8,128)(2,1)}, bf16[512,320]{1,0:T(8,128)(2,1)}, f32[8,384]{1,0:T(8,128)}, f32[8,384]{1,0:T(8,128)}) custom-call(bf16[512,320]{1,0:T(8,128)(2,1)} %bitcast.12, bf16[3,960,320]{2,1,0:T(8,128)(2,1)} %bitcast.10, bf16[3,960,320]{2,1,0:T(8,128)(2,1)} %bitcast.11, bf16[512,320]{1,0:T(8,128)(2,1)} %bitcast.13), custom_call_target="tpu_custom_call" | custom-call | tf_op jit(solution)/shard_map/conv_pair/pallas_call | solution.py:583
  56.4 2.0 %finish.1 = (bf16[512,320]{1,0:T(8,128)(2,1)}, bf16[512,320]{1,0:T(8,128)(2,1)}, f32[1800]{0:T(1024)}, f32[1800]{0:T(1024)}) custom-call(bf16[512,320]{1,0:T(8,128)(2,1)} %get-tuple-element.12.out_hbm, bf16[512,320]{1,0:T(8,128)(2,1)} %get-tuple-element.13.lg_hbm, f32[8,384]{1,0:T(8,128)} %get-tuple-element.14.g1_hbm, f32[8,384]{1,0:T(8,128)} %get-tuple-element.15.g2_hbm), custom_call_target="tpu_custom_call" | custom-call | tf_op jit(solution)/shard_map/finish/pallas_call | solution.py:646
